TPU v7x, 1024 devices: a whole 4x8x16 slice. The times are simulated.
1024 devices in a mesh: map: 128 (over z, y_lo, core), layer: 8 (over x, y_hi).
Axes of the slice: x: 4, y: 8 (y_hi: 2, y_lo: 4; y = y_hi * 4 + y_lo), z: 16, core: 2. Of those that a mesh axis runs over, the one named last changes fastest.
Arguments:
- velocity_init: float32 [2, 32, 256, 2048], P(None, 'layer', 'map'), may hold values from -4 to 4
- driving: float32 [2, 256, 2048], P(None, 'map', 'layer'), may hold values from -80 to 80
- observed: float32 [2, 256, 2048], P(None, 'map', 'layer'), may hold values from -4 to 4
- log_friction: float32 [256, 2048], P('map', 'layer'), may hold values from -1 to 1.5
- ice_mask: int32 [256, 2048], P('map', 'layer'), may hold values from 0 to 2
Outputs:
- velocity: float32 [2, 32, 256, 2048], P(None, 'layer', 'map')
- friction_new: float32 [256, 2048], P('map', 'layer')
- misfit: float32 [], replicated
All inputs are finite; a program needn't handle non-finite values.
Results may differ from a plain program's by a relative error of at most 0.0003.
Values sent between devices are 32-bit elements; how exact they have to be, the bound alone decides.
A program may use at most 32 MiB of HBM per device.

v0:
```python
import jax
import jax.numpy as jnp
from jax import lax
from jax.sharding import PartitionSpec as P

strain_floor = 0.1
step_size = 0.5


def with_halo(block, sides, width):
    for axis, dim in sides:
        count = lax.axis_size(axis)
        forward = [(i, i + 1) for i in range(count - 1)]
        backward = [(target, source) for source, target in forward]
        low = lax.ppermute(
            lax.slice_in_dim(block, block.shape[dim] - width, None, axis=dim), axis, forward
        )
        high = lax.ppermute(lax.slice_in_dim(block, 0, width, axis=dim), axis, backward)
        block = jnp.concatenate([low, block, high], axis=dim)
    return block


def viscosity_of(extended):
    along_x = extended[0]
    along_y = extended[1]
    stretch_x = (along_x[:, 2:, 1:-1] - along_x[:, :-2, 1:-1]) * 0.5
    shear_uy = (along_x[:, 1:-1, 2:] - along_x[:, 1:-1, :-2]) * 0.5
    shear_vx = (along_y[:, 2:, 1:-1] - along_y[:, :-2, 1:-1]) * 0.5
    stretch_y = (along_y[:, 1:-1, 2:] - along_y[:, 1:-1, :-2]) * 0.5
    shearing = shear_uy + shear_vx
    strain_rate = (
        stretch_x * stretch_x
        + stretch_y * stretch_y
        + stretch_x * stretch_y
        + 0.25 * shearing * shearing
    )
    return jnp.power(strain_floor + strain_rate, -1.0 / 3.0)


def face_terms(viscous):
    centre = viscous[:, 1:-1, 1:-1]
    east_face = 0.5 * (centre + viscous[:, 2:, 1:-1])
    west_face = 0.5 * (centre + viscous[:, :-2, 1:-1])
    north_face = 0.5 * (centre + viscous[:, 1:-1, 2:])
    south_face = 0.5 * (centre + viscous[:, 1:-1, :-2])
    return (east_face, west_face, north_face, south_face)


def horizontal_diag(face_list):
    east_face, west_face, north_face, south_face = face_list
    first = 4.0 * (east_face + west_face) + (north_face + south_face)
    second = east_face + west_face + 4.0 * (north_face + south_face)
    return jnp.stack([first, second], 0)


def neighbour_sum(face_list, extended):
    east_face, west_face, north_face, south_face = face_list
    comp_u = extended[0]
    comp_v = extended[1]
    first = (
        4.0 * (east_face * comp_u[:, 2:, 1:-1] + west_face * comp_u[:, :-2, 1:-1])
        + north_face * comp_u[:, 1:-1, 2:]
        + south_face * comp_u[:, 1:-1, :-2]
    )
    second = (
        east_face * comp_v[:, 2:, 1:-1]
        + west_face * comp_v[:, :-2, 1:-1]
        + 4.0 * (north_face * comp_v[:, 1:-1, 2:] + south_face * comp_v[:, 1:-1, :-2])
    )
    return jnp.stack([first, second], 0)


def column_solve(centre, side_diag, right_hand, friction):
    layer_total = centre.shape[0]
    vertical_gain = 2.0 * float(layer_total * layer_total)
    coupling = vertical_gain * 0.5 * (centre[:-1] + centre[1:])
    zero_layer = jnp.zeros_like(centre[:1])
    lower_link = jnp.concatenate([zero_layer, coupling], 0)
    upper_link = jnp.concatenate([coupling, zero_layer], 0)
    bed_term = jnp.concatenate([friction[None], jnp.zeros_like(centre[1:])], 0)
    diagonal = (lower_link + upper_link + bed_term)[None] + side_diag
    diagonal = jnp.moveaxis(diagonal, 1, 0)
    right_side = jnp.moveaxis(right_hand, 1, 0)

    def forward(carried, layer_item):
        ratio_prev, value_prev = carried
        diag_layer, lower_layer, upper_layer, right_layer = layer_item
        pivots = diag_layer + lower_layer * ratio_prev
        ratio = -upper_layer / pivots
        value = (right_layer + lower_layer * value_prev) / pivots
        return ((ratio, value), (ratio, value))

    start = (jnp.zeros_like(right_side[0]), jnp.zeros_like(right_side[0]))
    final_pair, (ratios, values) = lax.scan(
        forward, start, (diagonal, lower_link, upper_link, right_side), unroll=8
    )

    def backward(following, layer_item):
        ratio, value = layer_item
        current = value - ratio * following
        return (current, current)

    final_row, solved = lax.scan(
        backward, jnp.zeros_like(right_side[0]), (ratios, values), reverse=True, unroll=8
    )
    return jnp.moveaxis(solved, 0, 1)


def top_source(mismatch, layer_count):
    zero_part = jnp.zeros((2, layer_count - 1) + mismatch.shape[1:], jnp.float32)
    return jnp.concatenate([zero_part, (float(layer_count) * mismatch)[:, None]], 1)


def to_layers(columns):
    return lax.all_to_all(columns, "layer", split_axis=1, concat_axis=3, tiled=True)


def on_device(velocity_init, driving, observed, log_friction, ice_mask):
    ice_cols = ice_mask != 0
    friction = jnp.exp(log_friction) * (ice_mask == 1).astype(jnp.float32)
    forcing = driving[:, None]
    column_count = (
        log_friction.shape[0]
        * log_friction.shape[1]
        * lax.axis_size("map")
        * lax.axis_size("layer")
    )
    layers = velocity_init
    for iteration in range(2):
        padded = with_halo(layers, (("map", 2),), 2)
        padded = jnp.pad(padded, ((0, 0), (0, 0), (0, 0), (2, 2)))
        viscous = viscosity_of(padded)
        face_list = face_terms(viscous)
        column_pack = jnp.concatenate(
            [
                viscous[None, :, 1:-1, 1:-1],
                horizontal_diag(face_list),
                neighbour_sum(face_list, padded[:, :, 1:-1, 1:-1]),
            ],
            0,
        )
        columns = lax.all_to_all(column_pack, "layer", split_axis=3, concat_axis=1, tiled=True)
        centre = columns[0]
        side_diag = columns[1:3]
        velocity_cols = jnp.where(
            ice_cols, column_solve(centre, side_diag, forcing + columns[3:5], friction), 0.0
        )
        layers = to_layers(velocity_cols)
    mismatch = jnp.where(ice_cols, velocity_cols[:, -1] - observed, 0.0)
    source = top_source(mismatch, velocity_cols.shape[1])
    adjoint = jnp.where(ice_cols, column_solve(centre, side_diag, source, friction), 0.0)
    adjoint_layers = to_layers(adjoint)
    adjoint_rim = with_halo(adjoint_layers, (("map", 2),), 1)
    adjoint_rim = jnp.pad(adjoint_rim, ((0, 0), (0, 0), (0, 0), (1, 1)))
    side_terms = lax.all_to_all(
        neighbour_sum(face_list, adjoint_rim), "layer", split_axis=3, concat_axis=1, tiled=True
    )
    adjoint = jnp.where(
        ice_cols, column_solve(centre, side_diag, source + side_terms, friction), 0.0
    )
    gradient = -friction * (
        velocity_cols[0, 0] * adjoint[0, 0] + velocity_cols[1, 0] * adjoint[1, 0]
    )
    misfit_sum, grad_sum = lax.psum(
        (0.5 * jnp.sum(mismatch * mismatch), jnp.sum(gradient * gradient)), ("map", "layer")
    )
    grad_scale = jnp.sqrt(grad_sum / column_count + 1e-06)
    return (layers, log_friction - step_size * gradient / grad_scale, misfit_sum / column_count)


def solution(mesh):
    in_specs = (
        P(None, "layer", "map", None),
        P(None, "map", "layer"),
        P(None, "map", "layer"),
        P("map", "layer"),
        P("map", "layer"),
    )
    out_specs = (P(None, "layer", "map", None), P("map", "layer"), P())
    return jax.shard_map(
        on_device, mesh=mesh, in_specs=in_specs, out_specs=out_specs, check_vma=False
    )
```

profile of v0, /device:TPU:1, one launch (start us, length us, event | category | flops | bytes accessed | tf_op | source)
XLA Modules:
  0.0 383.4 jit_solution(18085656712427387291)
XLA Ops:
  1.6 4.6 %collective-permute-start = (f32[2,4,2,2048]{3,1,2,0:T(4,128)S(1)}, f32[2,4,2,2048]{3,1,2,0:T(4,128)S(1)}, u32[]{:S(2)}, u32[]{:S(2)}) collective-permute-start(f32[2,4,2,2048]{3,1,2,0:T(4,128)S(1)} %copy.78), channel_id=1, source_target_pairs={{0,8},{8,16},{16,24},{24,32},{32,40},{40,48},{48,56},{56,64},{64,7... | collective-permute-start | bytes 393224 | tf_op jit(solution)/shard_map/ppermute | solution.py:15
  6.2 12.8 %collective-permute-start.1 = (f32[2,4,2,2048]{3,1,2,0:T(4,128)S(1)}, f32[2,4,2,2048]{3,1,2,0:T(4,128)S(1)}, u32[]{:S(2)}, u32[]{:S(2)}) collective-permute-start(f32[2,4,2,2048]{3,1,2,0:T(4,128)S(1)} %copy.78), channel_id=1, source_target_pairs={{8,0},{16,8},{24,16},{32,24},{40,32},{48,40},{56,48},{64,56},{72,6... | collective-permute-start | bytes 393224 | tf_op jit(solution)/shard_map/ppermute | solution.py:18
  21.9 5.9 %copy.81 = f32[5,4,2,2048]{0,1,2,3:T(4,128)} copy(f32[5,4,2,2048]{3,1,2,0:T(4,128)S(1)} %fusion.422) | data formatting | bytes 655360 | tf_op jit(solution)/shard_map/concatenate | solution.py:134
  27.8 11.0 %reshape.658 = f32[8,1,10240]{2,1,0:T(1,128)} reshape(f32[2048,2,4,5]{3,2,1,0:T(4,128)} %bitcast.1644) | data formatting | bytes 655360
  38.8 3.6 all-to-all-start
  42.5 11.3 %all-to-all-done = f32[8,1,10240]{2,1,0:T(1,128)S(1)} async-done(((f32[8,1,10240]{2,1,0:T(1,128)}), f32[8,1,10240]{2,1,0:T(1,128)S(1)}, u32[]{:S(2)}, u32[]{:S(2)}) %all-to-all-start) | async-done | bytes 327712 | tf_op jit(solution)/shard_map/all_to_all | solution.py:142
  55.8 14.3 %reshape.659 = f32[2048,2,4,5]{3,2,1,0:T(4,128)} reshape(f32[8,10240]{1,0:T(8,128)S(1)} %reduce) | data formatting | bytes 655360
  70.1 6.8 %copy.82 = f32[5,4,2,8,256]{4,2,1,3,0:T(2,128)S(1)} copy(f32[5,4,2,8,256]{0,1,2,4,3:T(4,128)} %bitcast.1645) | data formatting | bytes 655360 | tf_op jit(solution)/shard_map/all_to_all | solution.py:142
  77.2 1.8 while.136
  79.9 14.6 %all_to_all.102 = f32[2,32,2,256]{3,2,0,1:T(2,128)S(1)} all-to-all(f32[2,32,2,256]{3,2,0,1:T(2,128)S(1)} %bitcast.1665), channel_id=1, replica_groups=mesh['map'=128,'layer'=8] {'layer'}, dimensions={1} | all-to-all | bytes 262144 | tf_op jit(solution)/shard_map/all_to_all | solution.py:115
  94.7 1.9 collective-permute-start.2
  96.6 4.4 %collective-permute-start.3 = (f32[2,4,2,2048]{3,1,2,0:T(4,128)S(1)}, f32[2,4,2,2048]{3,1,2,0:T(4,128)S(1)}, u32[]{:S(2)}, u32[]{:S(2)}) collective-permute-start(f32[2,4,2,2048]{3,1,2,0:T(4,128)S(1)} %all_to_all.80), channel_id=1, source_target_pairs={{8,0},{16,8},{24,16},{32,24},{40,32},{48,40},{56,48},{64,56},{72,6... | collective-permute-start | bytes 393224 | tf_op jit(solution)/shard_map/ppermute | solution.py:18
  101.0 1.9 collective-permute-done.3
  104.8 5.9 %copy.86 = f32[5,4,2,2048]{0,1,2,3:T(4,128)} copy(f32[5,4,2,2048]{3,1,2,0:T(4,128)S(1)} %fusion.406) | data formatting | bytes 655360 | tf_op jit(solution)/shard_map/concatenate | solution.py:134
  110.7 11.0 %reshape.660 = f32[8,1,10240]{2,1,0:T(1,128)} reshape(f32[2048,2,4,5]{3,2,1,0:T(4,128)} %bitcast.1646) | data formatting | bytes 655360
  121.8 3.4 all-to-all-start.2
  125.3 11.8 %all-to-all-done.2 = f32[8,1,10240]{2,1,0:T(1,128)S(1)} async-done(((f32[8,1,10240]{2,1,0:T(1,128)}), f32[8,1,10240]{2,1,0:T(1,128)S(1)}, u32[]{:S(2)}, u32[]{:S(2)}) %all-to-all-start.2) | async-done | bytes 327712 | tf_op jit(solution)/shard_map/all_to_all | solution.py:142
  138.4 14.3 %reshape.661 = f32[2048,2,4,5]{3,2,1,0:T(4,128)} reshape(f32[8,10240]{1,0:T(8,128)S(1)} %reduce.1) | data formatting | bytes 655360
  152.7 6.9 %copy.87 = f32[5,4,2,8,256]{4,2,1,3,0:T(2,128)S(1)} copy(f32[5,4,2,8,256]{0,1,2,4,3:T(4,128)} %bitcast.1647) | data formatting | bytes 655360 | tf_op jit(solution)/shard_map/all_to_all | solution.py:142
  159.9 1.8 while.138
  167.4 14.6 %all_to_all.103 = f32[2,32,2,256]{3,2,0,1:T(2,128)S(1)} all-to-all(f32[2,32,2,256]{3,2,0,1:T(2,128)S(1)} %bitcast.1667), channel_id=1, replica_groups=mesh['map'=128,'layer'=8] {'layer'}, dimensions={1} | all-to-all | bytes 262144 | tf_op jit(solution)/shard_map/all_to_all | solution.py:115
  182.1 1.9 collective-permute-start.4
  184.1 3.0 collective-permute-start.5
  187.1 3.6 all-to-all-start.3
  191.3 4.4 %copy.92 = f32[2,4,2,2048]{1,2,0,3:T(2,128)} copy(f32[2,4,2,2048]{3,1,2,0:T(4,128)S(1)} %pad_maximum_fusion) | data formatting | bytes 262144 | tf_op jit(solution)/shard_map/stack | solution.py:70
  195.7 8.6 %reshape.662 = f32[8,1,4096]{2,1,0:T(1,128)} reshape(f32[2048,2,2,4]{3,2,1,0:T(2,128)} %bitcast.1648) | data formatting | bytes 262144
  204.3 8.7 %all-to-all-start.5 = ((f32[8,1,4096]{2,1,0:T(1,128)}), f32[8,1,4096]{2,1,0:T(1,128)S(1)}, u32[]{:S(2)}, u32[]{:S(2)}) async-start(f32[8,1,4096]{2,1,0:T(1,128)} %reshape.662), calls=%async_computation.5 | async-start | bytes 262144 | tf_op jit(solution)/shard_map/all_to_all | solution.py:155
  214.5 8.6 %all-to-all-done.5 = f32[8,1,4096]{2,1,0:T(1,128)S(1)} async-done(((f32[8,1,4096]{2,1,0:T(1,128)}), f32[8,1,4096]{2,1,0:T(1,128)S(1)}, u32[]{:S(2)}, u32[]{:S(2)}) %all-to-all-start.5) | async-done | bytes 131104 | tf_op jit(solution)/shard_map/all_to_all | solution.py:155
  224.0 8.4 %reshape.663 = f32[2048,2,2,4]{3,2,1,0:T(2,128)} reshape(f32[8,4096]{1,0:T(8,128)S(1)} %reduce.2) | data formatting | bytes 262144
  232.4 5.2 %copy.93 = f32[2,4,2,8,256]{4,2,0,1,3:T(2,128)S(1)} copy(f32[2,4,2,8,256]{1,2,0,4,3:T(2,128)} %bitcast.1649) | data formatting | bytes 262144 | tf_op jit(solution)/shard_map/all_to_all | solution.py:155
  237.7 1.8 while.142
  241.7 138.6 %all-reduce.9 = (f32[]{:T(128)}, f32[]{:T(128)}) all-reduce(f32[]{:T(128)} %get-tuple-element.1115, f32[]{:T(128)S(6)} %mul.1092), channel_id=1, replica_groups=mesh['map'=128,'layer'=8] {'map','layer'}, use_global_device_ids=true, to_apply=%region_17.18 | all-reduce | flops 2 | bytes 16 | tf_op jit(solution)/shard_map/psum | solution.py:164
  (452 shorter events, 29.6 us)
Async XLA Ops:
  1.6 17.4 %collective-permute-start = (f32[2,4,2,2048]{3,1,2,0:T(4,128)S(1)}, f32[2,4,2,2048]{3,1,2,0:T(4,128)S(1)}, u32[]{:S(2)}, u32[]{:S(2)}) collective-permute-start(f32[2,4,2,2048]{3,1,2,0:T(4,128)S(1)} %copy.78), channel_id=1, source_target_pairs={{0,8},{8,16},{16,24},{24,32},{32,40},{40,48},{48,56},{56,64},{64,7... | collective-permute-start | bytes 393224 | tf_op jit(solution)/shard_map/ppermute | solution.py:15
  6.2 13.7 %collective-permute-start.1 = (f32[2,4,2,2048]{3,1,2,0:T(4,128)S(1)}, f32[2,4,2,2048]{3,1,2,0:T(4,128)S(1)}, u32[]{:S(2)}, u32[]{:S(2)}) collective-permute-start(f32[2,4,2,2048]{3,1,2,0:T(4,128)S(1)} %copy.78), channel_id=1, source_target_pairs={{8,0},{16,8},{24,16},{32,24},{40,32},{48,40},{56,48},{64,56},{72,6... | collective-permute-start | bytes 393224 | tf_op jit(solution)/shard_map/ppermute | solution.py:18
  21.9 20.6 %copy-start = (s32[2,256]{1,0:T(2,128)S(1)}, s32[2,256]{1,0:T(2,128)}, u32[]{:S(2)}) copy-start(s32[2,256]{1,0:T(2,128)} %param.25) | copy-start | bytes 6148
  21.9 20.6 %copy-start.1 = (f32[2,256]{1,0:T(2,128)S(1)}, f32[2,256]{1,0:T(2,128)}, u32[]{:S(2)}) copy-start(f32[2,256]{1,0:T(2,128)} %param.24) | copy-start | bytes 6148
  38.8 15.0 %all-to-all-start = ((f32[8,1,10240]{2,1,0:T(1,128)}), f32[8,1,10240]{2,1,0:T(1,128)S(1)}, u32[]{:S(2)}, u32[]{:S(2)}) async-start(f32[8,1,10240]{2,1,0:T(1,128)} %reshape.658), calls=%async_computation | async-start | bytes 655360 | tf_op jit(solution)/shard_map/all_to_all | solution.py:142
  55.7 21.4 %copy-start.2 = (f32[2,2,256]{2,1,0:T(2,128)S(1)}, f32[2,2,256]{2,1,0:T(2,128)}, u32[]{:S(2)}) copy-start(f32[2,2,256]{2,1,0:T(2,128)} %param.22) | copy-start | bytes 12292
  94.7 6.3 %collective-permute-start.2 = (f32[2,4,2,2048]{3,1,2,0:T(4,128)S(1)}, f32[2,4,2,2048]{3,1,2,0:T(4,128)S(1)}, u32[]{:S(2)}, u32[]{:S(2)}) collective-permute-start(f32[2,4,2,2048]{3,1,2,0:T(4,128)S(1)} %all_to_all.80), channel_id=1, source_target_pairs={{0,8},{8,16},{16,24},{24,32},{32,40},{40,48},{48,56},{56,64},{64,7... | collective-permute-start | bytes 393224 | tf_op jit(solution)/shard_map/ppermute | solution.py:15
  96.6 6.3 %collective-permute-start.3 = (f32[2,4,2,2048]{3,1,2,0:T(4,128)S(1)}, f32[2,4,2,2048]{3,1,2,0:T(4,128)S(1)}, u32[]{:S(2)}, u32[]{:S(2)}) collective-permute-start(f32[2,4,2,2048]{3,1,2,0:T(4,128)S(1)} %all_to_all.80), channel_id=1, source_target_pairs={{8,0},{16,8},{24,16},{32,24},{40,32},{48,40},{56,48},{64,56},{72,6... | collective-permute-start | bytes 393224 | tf_op jit(solution)/shard_map/ppermute | solution.py:18
  121.8 15.3 %all-to-all-start.2 = ((f32[8,1,10240]{2,1,0:T(1,128)}), f32[8,1,10240]{2,1,0:T(1,128)S(1)}, u32[]{:S(2)}, u32[]{:S(2)}) async-start(f32[8,1,10240]{2,1,0:T(1,128)} %reshape.660), calls=%async_computation.2 | async-start | bytes 655360 | tf_op jit(solution)/shard_map/all_to_all | solution.py:142
  152.7 10.5 %copy-start.3 = (f32[2,2,256]{2,1,0:T(2,128)S(1)}, f32[2,2,256]{2,1,0:T(2,128)}, u32[]{:S(2)}) copy-start(f32[2,2,256]{2,1,0:T(2,128)} %param.23) | copy-start | bytes 12292
  182.1 8.6 %collective-permute-start.4 = (f32[2,4,1,2048]{3,1,2,0:T(4,128)S(1)}, f32[2,4,1,2048]{3,1,2,0:T(4,128)S(1)}, u32[]{:S(2)}, u32[]{:S(2)}) collective-permute-start(f32[2,4,1,2048]{3,1,2,0:T(4,128)S(1)} %get-tuple-element.1241), channel_id=1, source_target_pairs={{0,8},{8,16},{16,24},{24,32},{32,40},{40,48},{48,56},{56,64},{64,7... | collective-permute-start | bytes 196616 | tf_op jit(solution)/shard_map/ppermute | solution.py:15
  184.1 6.7 %collective-permute-start.5 = (f32[2,4,1,2048]{3,1,2,0:T(4,128)S(1)}, f32[2,4,1,2048]{3,1,2,0:T(4,128)S(1)}, u32[]{:S(2)}, u32[]{:S(2)}) collective-permute-start(f32[2,4,1,2048]{3,1,2,0:T(4,128)S(1)} %get-tuple-element.1242), channel_id=1, source_target_pairs={{8,0},{16,8},{24,16},{32,24},{40,32},{48,40},{56,48},{64,56},{72,6... | collective-permute-start | bytes 196616 | tf_op jit(solution)/shard_map/ppermute | solution.py:18
  187.1 17.2 %all-to-all-start.3 = ((f32[2,32,2,256]{3,2,0,1:T(2,128)}), f32[2,32,2,256]{3,2,0,1:T(2,128)S(1)}, u32[]{:S(2)}, u32[]{:S(2)}) async-start(f32[2,32,2,256]{3,2,0,1:T(2,128)} %bitcast.46), calls=%async_computation.3 | async-start | bytes 262144 | tf_op jit(solution)/shard_map/all_to_all | solution.py:115
  204.3 18.8 %all-to-all-start.5 = ((f32[8,1,4096]{2,1,0:T(1,128)}), f32[8,1,4096]{2,1,0:T(1,128)S(1)}, u32[]{:S(2)}, u32[]{:S(2)}) async-start(f32[8,1,4096]{2,1,0:T(1,128)} %reshape.662), calls=%async_computation.5 | async-start | bytes 262144 | tf_op jit(solution)/shard_map/all_to_all | solution.py:155
where the time goes:
time: 385 us; the launch traced here: 383 us
  blocking collectives  168 us (44%)
  local copies, waits for them, and re-layouts  109 us (28%)
  starting transfers between devices  48 us (12%)
  waiting for transfers between devices  34.6 us (9%)
  other arithmetic  17.9 us (5%)
  between operations  4.47 us (1%)
    psum x1, blocking collectives, on_device(): lax.psum((0.5 * jnp.sum(mismatch * mismatch), jnp.sum(gradient * gradient...  139 us
    unnamed x17, local copies, waits for them, and re-layouts  68.8 us
    all_to_all x2, blocking collectives, to_layers(): lax.all_to_all(columns, 'layer', split_axis=1, concat_axis=3, tiled=True)  29.2 us
    all_to_all x2, waiting for transfers between devices, on_device(): lax.all_to_all(column_pack, 'layer', split_axis=3, concat_axis=1, tiled=T...  23.1 us
    ppermute x3, starting transfers between devices, with_halo(): lax.ppermute(lax.slice_in_dim(block, 0, width, axis=dim), axis, backward)  20.2 us
    all_to_all x3, local copies, waits for them, and re-layouts, on_device(): lax.all_to_all(column_pack, 'layer', split_axis=3, concat_axis=1, tiled=T...  14.2 us
    concatenate x2, local copies, waits for them, and re-layouts, on_device(): jnp.concatenate([viscous[None, :, 1:-1, 1:-1], horizontal_diag(face_list)...  11.9 us
    all_to_all x1, starting transfers between devices, on_device(): lax.all_to_all(neighbour_sum(face_list, adjoint_rim), 'layer', split_axis...  8.7 us
  transfers between devices with their start and end apart: 10, of which 5 were waited for; matrix products, arithmetic and copies ran while one was open for 4% of the time, Pallas kernels for 0%

commit v1 on v0

v1 whole, which is shorter than its diff:
```python
import jax
import jax.numpy as jnp
from jax import lax
from jax.experimental import pallas as pl
from jax.experimental.pallas import tpu as pltpu
from jax.sharding import PartitionSpec as P

strain_floor = 0.1
step_size = 0.5
LAYERS = 32
SLOTS = 8
BLOCKS = 128
GROUPS = 4
COLUMNS = 256 * 2048
MESH = pl.DeviceIdType.MESH
f32 = jnp.float32


def place(m):
    return lax.div(m, 8), lax.rem(lax.div(m, 2), 4), lax.rem(m, 2)


def device_at(x, y, z, core):
    return ((z * 4 + lax.rem(y, 4)) * 2 + core, x * 2 + lax.div(y, 4))


def owner_of(m, l):
    z, y_lo, core = place(m)
    y = lax.rem(l, 2) * 4 + y_lo
    odd = lax.rem(z, 2)
    return device_at(lax.div(l, 2), lax.rem((1 - odd) * (y + 2) + odd * (13 - y), 8), z, core)


def block_of(x, y, z, core):
    odd = lax.rem(z, 2)
    return device_at(x, lax.rem((1 - odd) * (y + 6) + odd * (13 - y), 8), z, core)


def kernel(
    vel_hbm, drv_hbm, obs_hbm, logf_hbm, mask_hbm,
    out_hbm, fric_out, misfit_out,
    vin, drv, obs, logf, mask, stage_main, stage_rim, small, small_in,
    w0m, w0r, w1m, w1r, w2m, w2r, dnm, dnr, upm, upr, dnm1, dnr1, upm1, upr1,
    am, ar, adn, aup,
    eta_m, eta_r, diag_m, diag_r, rhs_m, rhs_r, ratio_m, ratio_r, val_m, val_r, inv_m, inv_r, rim_x, faces,
    vel_in, vout, grad, grad_in,
    row1, row2, row3, sum1, sum2, sum3,
    load_sem, out_sem, a2a_send, a2a_recv, small_send, small_recv, halo_send, halo_recv,
    vel_send, vel_recv, grad_send, grad_recv,
    s1_send, s1_recv, s2_send, s2_recv, s3_send, s3_recv,
):
    M = lax.axis_index("map")
    L = lax.axis_index("layer")
    z, y_lo, core = place(M)
    x = lax.div(L, 2)
    y = lax.rem(L, 2) * 4 + y_lo
    bm, bl = block_of(x, y, z, core)
    below = owner_of(lax.rem(bm + BLOCKS - 1, BLOCKS), bl)
    above = owner_of(lax.rem(bm + 1, BLOCKS), bl)
    owners = [owner_of(M, jnp.int32(l)) for l in range(SLOTS)]
    holders = [(bm, jnp.int32(l)) for l in range(SLOTS)]
    me1, me2, me3 = x * 2 + core, y, z

    def peer1(j):
        return device_at(lax.div(j, 2), y, z, lax.rem(j, 2))

    def peer2(j):
        return device_at(x, j, z, core)

    def peer3(j):
        return device_at(x, y, j, core)

    stages = (
        (8, me1, peer1, row1, sum1, s1_send, s1_recv),
        (8, me2, peer2, row2, sum2, s2_send, s2_recv),
        (16, me3, peer3, row3, sum3, s3_send, s3_recv),
    )
    partners = []
    for count, me, peer, *_ in reversed(stages):
        partners += [peer(lax.rem(me + i, count)) for i in range(1, count)]
    partners += owners + holders + [below, above]
    barrier = pltpu.get_barrier_semaphore()
    for partner in partners:
        pl.semaphore_signal(barrier, inc=1, device_id=partner, device_id_type=MESH)

    loads = [
        pltpu.make_async_copy(src, dst, load_sem.at[i])
        for i, (src, dst) in enumerate(
            ((vel_hbm, vin), (drv_hbm, drv), (obs_hbm, obs), (logf_hbm, logf), (mask_hbm, mask))
        )
    ]
    for load in loads:
        load.start()
    for load in loads[1:]:
        load.wait()
    small[0:8, :] = drv[...]
    small[8:16, :] = obs[...]
    small[16:20, :] = jnp.exp(logf[...]) * (mask[...] == 1).astype(f32)
    small[20:24, :] = (mask[...] != 0).astype(f32)
    loads[0].wait()

    lane2 = lax.broadcasted_iota(jnp.int32, (2, 128), 1)
    zero2 = jnp.zeros((2, 128), f32)
    for c in range(2):
        for kk in range(4):
            base = (c * 4 + kk) * 32
            for l in range(SLOTS):
                at = l * 32 + kk * 8 + c * 4
                stage_main[at:at + 4, :] = vin[base + l * 4:base + l * 4 + 4, :]
                right = vin[base + l * 4 + 4:base + l * 4 + 6, :] if l < SLOTS - 1 else zero2
                left = vin[base + l * 4 - 2:base + l * 4, :] if l > 0 else zero2
                at = l * 16 + kk * 4 + c * 2
                stage_rim[at:at + 2, :] = jnp.where(lane2 < 64, right, left)

    pl.semaphore_wait(barrier, len(partners))

    sends = []

    def remote(src, dst, send_sem, recv_sem, device):
        copy = pltpu.make_async_remote_copy(
            src_ref=src, dst_ref=dst, send_sem=send_sem, recv_sem=recv_sem, device_id=device, device_id_type=MESH
        )
        copy.start()
        sends.append(copy)

    def arrived(ref, sem):
        pltpu.make_async_copy(ref, ref, sem).wait()

    rows_main = pl.ds(pl.multiple_of(L * 32, 32), 32)
    rows_rim = pl.ds(pl.multiple_of(L * 16, 16), 16)
    for l in range(SLOTS):
        remote(stage_main.at[l * 32:l * 32 + 32], w0m.at[rows_main], a2a_send.at[0, l], a2a_recv.at[0, L], owners[l])
        remote(stage_rim.at[l * 16:l * 16 + 16], w0r.at[rows_rim], a2a_send.at[1, l], a2a_recv.at[1, L], owners[l])
    for side in range(3):
        target = owner_of(M, lax.rem(L + SLOTS + 1 - side, SLOTS))
        remote(small, small_in.at[side], small_send.at[side], small_recv.at[side], target)

    for l in range(SLOTS):
        rm, rr = pl.ds(l * 32, 32), pl.ds(l * 16, 16)
        arrived(w0m.at[rm], a2a_recv.at[0, l])
        arrived(w0r.at[rr], a2a_recv.at[1, l])
        for i, (device, mains, rims) in enumerate(((below, upm, upr), (above, dnm, dnr))):
            for part, src, dst, rows in ((0, w0m, mains, rm), (1, w0r, rims, rr)):
                pltpu.make_async_remote_copy(
                    src_ref=src.at[rows], dst_ref=dst.at[rows], send_sem=halo_send.at[0, i, part],
                    recv_sem=halo_recv.at[0, i, part], device_id=device, device_id_type=MESH,
                ).start()

    for side in range(3):
        arrived(small_in.at[side], small_recv.at[side])
    lane4 = lax.broadcasted_iota(jnp.int32, (4, 128), 1)
    lane8 = lax.broadcasted_iota(jnp.int32, (8, 128), 1)
    has_left = (bl > 0).astype(f32)
    has_right = (bl < SLOTS - 1).astype(f32)
    has_below = (bm > 0).astype(f32)
    has_above = (bm < BLOCKS - 1).astype(f32)

    def double(rows):
        return jnp.concatenate([rows, rows], 0)

    def rim_rows(start, comps):
        parts = []
        for c in range(comps):
            at = start + 4 * c
            parts.append(jnp.where(lane2 < 64, small_in[2, at:at + 2, :] * has_right, small_in[0, at + 2:at + 4, :] * has_left))
        if comps == 1:
            parts = parts * 2
        return double(jnp.concatenate(parts, 0))

    drive = (small_in[1, 0:8, :], rim_rows(0, 2))
    seen = (small_in[1, 8:16, :], rim_rows(8, 2))
    bed = (double(small_in[1, 16:20, :]), rim_rows(16, 1))
    ice = (double(small_in[1, 20:24, :]) > 0.5, rim_rows(20, 1) > 0.5)

    def ahead(tiles):
        turned = [pltpu.roll(t, 127, 1) for t in tiles]
        return [jnp.where(lane8 == 127, turned[(i + 1) % 3], turned[i]) for i in range(3)]

    def behind(tiles):
        turned = [pltpu.roll(t, 1, 1) for t in tiles]
        return [jnp.where(lane8 == 0, turned[(i + 2) % 3], turned[i]) for i in range(3)]

    def load_tiles(main, rim, j, c, r):
        tiles = [main[pl.ds(j * 64 + (c * 4 + t * 2 + r), 8, stride=8), :] for t in range(2)]
        return tiles + [rim[pl.ds(j * 32 + (c * 2 + r), 8, stride=4), :]]

    def store_tile(main, rim, j, c, t, r, value):
        if t < 2:
            main[pl.ds(j * 64 + (c * 4 + t * 2 + r), 8, stride=8), :] = value
        else:
            rim[pl.ds(j * 64 + (c * 2 + r), 8, stride=8), :] = value

    def scaled(tiles, factor):
        return [t * factor for t in tiles]

    def forward_terms(own, low, high):
        def group(j, carry):
            w = []
            for c in range(2):
                rows = [scaled(load_tiles(*low, j, c, r), has_below) for r in range(2)]
                rows += [load_tiles(*own, j, c, r) for r in range(2)]
                rows += [scaled(load_tiles(*high, j, c, r), has_above) for r in range(2)]
                w.append(rows)
            right = [[ahead(w[c][r]) for r in range(1, 5)] for c in range(2)]
            left = [[behind(w[c][r]) for r in range(1, 5)] for c in range(2)]
            eta = []
            for r in range(4):
                tiles = []
                for t in range(3):
                    u_x = (w[0][r + 2][t] - w[0][r][t]) * 0.5
                    v_x = (w[1][r + 2][t] - w[1][r][t]) * 0.5
                    u_y = (right[0][r][t] - left[0][r][t]) * 0.5
                    v_y = (right[1][r][t] - left[1][r][t]) * 0.5
                    shear = u_y + v_x
                    rate = u_x * u_x + v_y * v_y + u_x * v_y + 0.25 * shear * shear
                    tiles.append(jnp.exp(jnp.log(strain_floor + rate) * (-1.0 / 3.0)))
                eta.append(tiles)
            for r in range(2):
                eta_right, eta_left = ahead(eta[r + 1]), behind(eta[r + 1])
                for t in range(3):
                    centre = eta[r + 1][t]
                    east = 0.5 * (centre + eta[r + 2][t])
                    west = 0.5 * (centre + eta[r][t])
                    north = 0.5 * (centre + eta_right[t])
                    south = 0.5 * (centre + eta_left[t])
                    along, across = east + west, north + south
                    if t < 2:
                        for i, face in enumerate((east, west, north, south)):
                            faces[j, (r * 2 + t) * 4 + i] = face
                    u, v = w
                    sum_u = (
                        4.0 * (east * u[r + 3][t] + west * u[r + 1][t])
                        + north * right[0][r + 1][t] + south * left[0][r + 1][t]
                    )
                    sum_v = (
                        east * v[r + 3][t] + west * v[r + 1][t]
                        + 4.0 * (north * right[1][r + 1][t] + south * left[1][r + 1][t])
                    )
                    store_tile(eta_m, eta_r, j, 0, t, r, centre)
                    store_tile(eta_m, eta_r, j, 1, t, r, centre)
                    store_tile(diag_m, diag_r, j, 0, t, r, 4.0 * along + across)
                    store_tile(diag_m, diag_r, j, 1, t, r, along + 4.0 * across)
                    store_tile(rhs_m, rhs_r, j, 0, t, r, sum_u)
                    store_tile(rhs_m, rhs_r, j, 1, t, r, sum_v)
            return carry

        lax.fori_loop(0, GROUPS, group, 0)

    pairs = (
        (eta_m, diag_m, rhs_m, ratio_m, val_m, inv_m),
        (eta_r, diag_r, rhs_r, ratio_r, val_r, inv_r),
    )

    def at(k):
        return pl.ds(pl.multiple_of(k * 8, 8), 8)

    def solve(out_main):
        def eliminate(k, carry, last=False):
            new = []
            for part in range(2):
                eta, diag, rhs, ratio, val, inv = pairs[part]
                lower, ratio_prev, val_prev, pad = carry[part]
                if last:
                    upper = jnp.zeros((8, 128), f32)
                else:
                    upper = 1024.0 * (eta[at(k), :] + eta[at(k + 1), :])
                inverse = 1.0 / (((lower + upper + pad) + diag[at(k), :]) + lower * ratio_prev)
                ratio_now = -upper * inverse
                val_now = (drive[part] + rhs[at(k), :] + lower * val_prev) * inverse
                ratio[at(k), :] = ratio_now
                val[at(k), :] = val_now
                inv[at(k), :] = inverse
                new.append((upper, ratio_now, val_now, jnp.zeros((8, 128), f32)))
            return tuple(new)

        zero = jnp.zeros((8, 128), f32)
        carry = tuple((zero, zero, zero, bed[part]) for part in range(2))
        carry = lax.fori_loop(0, LAYERS - 1, eliminate, carry)
        eliminate(LAYERS - 1, carry, last=True)
        outs = (out_main, rim_x)

        def substitute(i, following):
            k = LAYERS - 1 - i
            new = []
            for part in range(2):
                ratio, val = pairs[part][3], pairs[part][4]
                now = val[at(k), :] - ratio[at(k), :] * following[part]
                outs[part][at(k), :] = jnp.where(ice[part], now, 0.0)
                new.append(now)
            return tuple(new)

        lax.fori_loop(0, LAYERS, substitute, (zero, zero))

    def squeeze_rim(out_rim):
        for s in range(4):
            for j in range(GROUPS):
                out_rim[pl.ds(j * 32 + s, 8, stride=4), :] = rim_x[pl.ds(j * 64 + s, 8, stride=8), :]

    for i, (mains, rims) in enumerate(((upm, upr), (dnm, dnr))):
        arrived(mains, halo_recv.at[0, i, 0])
        arrived(rims, halo_recv.at[0, i, 1])
    forward_terms((w0m, w0r), (dnm, dnr), (upm, upr))
    solve(w1m)
    squeeze_rim(w1r)
    for i, (device, mains, rims) in enumerate(((below, upm1, upr1), (above, dnm1, dnr1))):
        remote(w1m, mains, halo_send.at[1, i, 0], halo_recv.at[1, i, 0], device)
        remote(w1r, rims, halo_send.at[1, i, 1], halo_recv.at[1, i, 1], device)

    for i, (mains, rims) in enumerate(((upm1, upr1), (dnm1, dnr1))):
        arrived(mains, halo_recv.at[1, i, 0])
        arrived(rims, halo_recv.at[1, i, 1])
    forward_terms((w1m, w1r), (dnm1, dnr1), (upm1, upr1))
    solve(w2m)

    top = LAYERS - 1
    tops = (w2m[at(top), :], rim_x[at(top), :])
    mismatch = [jnp.where(ice[part], tops[part] - seen[part], 0.0) for part in range(2)]
    source = [float(LAYERS) * mismatch[part] for part in range(2)]
    starts = tuple(source[part] * pairs[part][5][at(top), :] for part in range(2))
    adjoints = (am, rim_x)
    for part in range(2):
        adjoints[part][at(top), :] = jnp.where(ice[part], starts[part], 0.0)

    def substitute_first(i, following):
        k = LAYERS - 2 - i
        new = []
        for part in range(2):
            now = -pairs[part][3][at(k), :] * following[part]
            adjoints[part][at(k), :] = jnp.where(ice[part], now, 0.0)
            new.append(now)
        return tuple(new)

    lax.fori_loop(0, LAYERS - 1, substitute_first, starts)
    remote(am, aup, halo_send.at[2, 0, 0], halo_recv.at[2, 0, 0], below)
    remote(am, adn, halo_send.at[2, 1, 0], halo_recv.at[2, 1, 0], above)
    for l in range(SLOTS):
        remote(
            w2m.at[l * 32:l * 32 + 32], vel_in.at[pl.ds(pl.multiple_of(bl * 32, 32), 32)],
            vel_send.at[l], vel_recv.at[bl], holders[l],
        )
    squeeze_rim(ar)

    arrived(aup, halo_recv.at[2, 0, 0])
    arrived(adn, halo_recv.at[2, 1, 0])

    def adjoint_terms(j, carry):
        for c in range(2):
            rows = [load_tiles(am, ar, j, c, r) for r in range(2)]
            for r in range(2):
                right, left = ahead(rows[r]), behind(rows[r])
                for t in range(2):
                    if r == 0:
                        low = adn[pl.ds(j * 64 + (c * 4 + t * 2 + 1), 8, stride=8), :] * has_below
                        high = rows[1][t]
                    else:
                        low = rows[0][t]
                        high = aup[pl.ds(j * 64 + (c * 4 + t * 2), 8, stride=8), :] * has_above
                    east, west, north, south = [faces[j, (r * 2 + t) * 4 + i] for i in range(4)]
                    along = east * high + west * low
                    across = north * right[t] + south * left[t]
                    value = 4.0 * along + across if c == 0 else along + 4.0 * across
                    rhs_m[pl.ds(j * 64 + (c * 4 + t * 2 + r), 8, stride=8), :] = value
        return carry

    lax.fori_loop(0, GROUPS, adjoint_terms, 0)
    zero = jnp.zeros((8, 128), f32)
    rhs_m[at(top), :] = rhs_m[at(top), :] + source[0]

    def eliminate_second(k, prev):
        lower = 1024.0 * (eta_m[at(k - 1), :] + eta_m[at(k), :])
        now = (rhs_m[at(k), :] + lower * prev) * inv_m[at(k), :]
        val_m[at(k), :] = now
        return now

    first = rhs_m[0:8, :] * inv_m[0:8, :]
    val_m[0:8, :] = first
    lax.fori_loop(1, LAYERS, eliminate_second, first)

    def substitute_second(i, following):
        k = LAYERS - 1 - i
        return val_m[at(k), :] - ratio_m[at(k), :] * following

    bottom = jnp.where(ice[0], lax.fori_loop(0, LAYERS, substitute_second, zero), 0.0)

    product = w2m[0:8, :] * bottom
    gradient = -bed[0][0:4, :] * (product[0:4, :] + product[4:8, :])
    grad[...] = gradient
    remote(grad, grad_in, grad_send, grad_recv, (bm, bl))

    lane1 = lax.broadcasted_iota(jnp.int32, (1, 128), 1)
    grad_row = jnp.sum(gradient * gradient, axis=0, keepdims=True)
    fit_row = jnp.sum(0.5 * mismatch[0] * mismatch[0], axis=0, keepdims=True)
    grad_row = grad_row + pltpu.roll(grad_row, 64, 1)
    fit_row = fit_row + pltpu.roll(fit_row, 64, 1)
    row = jnp.where(lane1 < 64, grad_row, fit_row)
    for number, (count, me, peer, row_ref, sum_ref, send_sem, recv_sem) in enumerate(stages):
        row_ref[...] = row
        sum_ref[me] = row
        for i in range(1, count):
            other = lax.rem(me + i, count)
            remote(row_ref, sum_ref.at[me], send_sem.at[i], recv_sem.at[me], peer(other))
        if number == 1:
            for l in range(SLOTS):
                arrived(vel_in.at[l * 32:l * 32 + 32], vel_recv.at[l])
            for c in range(2):
                for kk in range(4):
                    for l in range(SLOTS):
                        to = (c * 4 + kk) * 32 + l * 4
                        vout[to:to + 4, :] = vel_in[l * 32 + kk * 8 + c * 4:l * 32 + kk * 8 + c * 4 + 4, :]
            store = pltpu.make_async_copy(vout, out_hbm, out_sem)
            store.start()
        for i in range(1, count):
            other = lax.rem(me + i, count)
            arrived(sum_ref.at[other], recv_sem.at[other])
        row = sum_ref[0]
        for i in range(1, count):
            row = row + sum_ref[i]

    grad_total = jnp.sum(jnp.where(lane1 < 64, row, 0.0))
    fit_total = jnp.sum(jnp.where(lane1 < 64, 0.0, row))
    misfit_out[0, 0] = fit_total / COLUMNS
    arrived(grad_in, grad_recv)
    scale = jnp.sqrt(jnp.full((4, 128), grad_total, f32) / COLUMNS + 1e-06)
    fric_out[...] = logf[...] - step_size * grad_in[...] / scale

    for copy in sends:
        copy.wait_send()
    for i in range(2):
        for part, src in ((0, w0m), (1, w0r)):
            arrived(src, halo_send.at[0, i, part])
    store.wait()


def on_device(velocity_init, driving, observed, log_friction, ice_mask):
    vel = velocity_init.reshape(2, 4, 2, 16, 128).transpose(0, 1, 3, 2, 4).reshape(256, 128)

    def tiles(a, lead):
        b = a.reshape(lead, 2, 2, 128).transpose(0, 2, 1, 3)
        return b.reshape(lead * 4, 128)

    full, half = (256, 128), (128, 128)
    vm = lambda shape: pltpu.VMEM(shape, f32)
    dma = pltpu.SemaphoreType.DMA
    scratch = [
        vm(full), vm((8, 128)), vm((8, 128)), vm((4, 128)), pltpu.VMEM((4, 128), jnp.int32),
        vm(full), vm(half), vm((24, 128)), vm((3, 24, 128)),
    ]
    scratch += [vm(full), vm(half)] * 3
    scratch += [vm(full), vm(half)] * 4
    scratch += [vm(full), vm(half), vm(full), vm(full)]
    scratch += [vm(full)] * 12 + [vm(full), vm((GROUPS, 16, 8, 128))]
    scratch += [vm(full), vm(full), vm((4, 128)), vm((4, 128))]
    scratch += [vm((1, 128))] * 3 + [vm((8, 1, 128)), vm((8, 1, 128)), vm((16, 1, 128))]
    scratch += [
        dma((5,)), dma, dma((2, 8)), dma((2, 8)), dma((3,)), dma((3,)), dma((3, 2, 2)), dma((3, 2, 2)),
        dma((8,)), dma((8,)), dma, dma,
        dma((8,)), dma((8,)), dma((8,)), dma((8,)), dma((16,)), dma((16,)),
    ]
    anywhere = pl.BlockSpec(memory_space=pl.ANY)
    out, fric, misfit = pl.pallas_call(
        kernel,
        out_shape=(
            jax.ShapeDtypeStruct(full, f32),
            jax.ShapeDtypeStruct((4, 128), f32),
            jax.ShapeDtypeStruct((1, 1), f32),
        ),
        in_specs=[anywhere] * 5,
        out_specs=(
            anywhere,
            pl.BlockSpec(memory_space=pltpu.VMEM),
            pl.BlockSpec(memory_space=pltpu.SMEM),
        ),
        scratch_shapes=scratch,
        compiler_params=pltpu.CompilerParams(collective_id=0, has_side_effects=True),
    )(vel, tiles(driving, 2), tiles(observed, 2), tiles(log_friction, 1), tiles(ice_mask, 1))
    velocity = out.reshape(2, 4, 16, 2, 128).transpose(0, 1, 3, 2, 4).reshape(2, 4, 2, 2048)
    fric = fric.reshape(2, 2, 128).transpose(1, 0, 2).reshape(2, 256)
    return velocity, fric, misfit.reshape(())


def solution(mesh):
    in_specs = (
        P(None, "layer", "map", None),
        P(None, "map", "layer"),
        P(None, "map", "layer"),
        P("map", "layer"),
        P("map", "layer"),
    )
    out_specs = (P(None, "layer", "map", None), P("map", "layer"), P())
    return jax.shard_map(on_device, mesh=mesh, in_specs=in_specs, out_specs=out_specs, check_vma=False)
```

time: 385 us -> 69.6 us (0.18)
  blocking collectives: 168 us -> 0 us
  local copies, waits for them, and re-layouts: 109 us -> 2.15 us
  Pallas kernels: 0 us -> 64.2 us
  starting transfers between devices: 48 us -> 0 us
  waiting for transfers between devices: 34.6 us -> 0 us
  other arithmetic: 17.9 us -> 0 us
    psum x1 -> x0, blocking collectives: 139 us -> none  [on_device(): lax.psum((0.5 * jnp.sum(mismatch * mismatch), jnp.sum(gradient * gradient...]
    unnamed x17 -> x4, local copies, waits for them, and re-layouts: 68.8 us -> 2.15 us
    pallas_call x0 -> x1, Pallas kernels: none -> 64.2 us  [on_device(): pl.pallas_call(kernel, out_shape=(jax.ShapeDtypeStruct(full, f32), jax.Sh...]
    all_to_all x4 -> x0, waiting for transfers between devices: 31.7 us -> none  [the longest x2 23.1 us: on_device(): lax.all_to_all(column_pack, 'layer', split_axis=3, concat_axis=1, tiled=T...]
    all_to_all x2 -> x0, blocking collectives: 29.2 us -> none  [to_layers(): lax.all_to_all(columns, 'layer', split_axis=1, concat_axis=3, tiled=True)]
    ppermute x6 -> x0, starting transfers between devices: 28.6 us -> none  [the longest x3 20.2 us: with_halo(): lax.ppermute(lax.slice_in_dim(block, 0, width, axis=dim), axis, backward)]
    all_to_all x10 -> x0, local copies, waits for them, and re-layouts: 20.6 us -> none  [the longest x3 14.2 us: on_device(): lax.all_to_all(column_pack, 'layer', split_axis=3, concat_axis=1, tiled=T...]
    all_to_all x4 -> x0, starting transfers between devices: 19.4 us -> none  [the longest x1 8.7 us: on_device(): lax.all_to_all(neighbour_sum(face_list, adjoint_rim), 'layer', split_axis...]
  transfers between devices with their start and end apart: 10 -> 0, of which waited for: 5 -> 0; matrix products, arithmetic and copies ran while one was open for 4% -> 0% of each run, Pallas kernels for 0% -> 0%
where the time goes in v1:
time: 69.6 us; the launch traced here: 68.8 us
  Pallas kernels  64.2 us (92%)
  between operations  2.41 us (3%)
  local copies, waits for them, and re-layouts  2.15 us (3%)
    pallas_call x1, Pallas kernels, on_device(): pl.pallas_call(kernel, out_shape=(jax.ShapeDtypeStruct(full, f32), jax.Sh...  64.2 us
    unnamed x4, local copies, waits for them, and re-layouts  2.15 us

profile of v1, /device:TPU:1, one launch (start us, length us, event | category | flops | bytes accessed | tf_op | source)
XLA Modules:
  0.0 68.8 jit_solution(11532358188158865195)
XLA Ops:
  0.6 64.2 %shard_map.76 = (f32[256,128]{1,0:T(8,128)}, f32[4,128]{1,0:T(4,128)}, f32[1,1]{1,0:T(1,128)}) custom-call(f32[256,128]{1,0:T(8,128)} %bitcast.36, f32[8,128]{1,0:T(8,128)} %bitcast.38, f32[8,128]{1,0:T(8,128)} %bitcast.39, f32[4,128]{1,0:T(4,128)} %bitcast.40, s32[4,128]{1,0:T(4,128)} %bitcast.41), custom_call_target="tpu_custom_call" | custom-call | tf_op jit(solution)/shard_map/pallas_call | solution.py:460
  64.9 0.0 copy-start
  64.9 1.6 %copy.18 = f32[2,4,2,2048]{3,2,1,0:T(2,128)} copy(f32[2,4,2,2048]{3,2,1,0:T(2,128)} %bitcast.37) | data formatting | bytes 262144
  66.4 0.0 copy-done
  66.4 0.6 copy.19
Async XLA Ops:
  64.9 1.6 %copy-start = (f32[4,128]{1,0:T(4,128)S(1)}, f32[4,128]{1,0:T(4,128)}, u32[]{:S(2)}) copy-start(f32[4,128]{1,0:T(4,128)} %get-tuple-element.7) | copy-start | bytes 6148

commit v2 on v1

v2 whole, which is shorter than its diff:
```python
import jax
import jax.numpy as jnp
from jax import lax
from jax.experimental import pallas as pl
from jax.experimental.pallas import tpu as pltpu
from jax.sharding import PartitionSpec as P

strain_floor = 0.1
step_size = 0.5
LAYERS = 32
SLOTS = 8
BLOCKS = 128
GROUPS = 4
COLUMNS = 256 * 2048
MESH = pl.DeviceIdType.MESH
f32 = jnp.float32

SLAB = 40


def place(m):
    return lax.div(m, 8), lax.rem(lax.div(m, 2), 4), lax.rem(m, 2)


def device_at(x, y, z, core):
    return ((z * 4 + lax.rem(y, 4)) * 2 + core, x * 2 + lax.div(y, 4))


def owner_of(m, l):
    z, y_lo, core = place(m)
    y = lax.rem(l, 2) * 4 + y_lo
    odd = lax.rem(z, 2)
    return device_at(lax.div(l, 2), lax.rem(odd * (y + 2) + (1 - odd) * (13 - y), 8), z, core)


def block_of(x, y, z, core):
    odd = lax.rem(z, 2)
    return device_at(x, lax.rem(odd * (y + 6) + (1 - odd) * (13 - y), 8), z, core)


def kernel(
    vel_hbm, drv_hbm, obs_hbm, logf_hbm, mask_hbm,
    out_hbm, fric_out, misfit_out,
    vin, drv, obs, logf, mask, stage, small, small_in,
    w0, w1, w2, dn0, up0, dn1, up1, am, adn, aup, alow, ahigh,
    eta_m, eta_r, diag_m, diag_r, rhs_m, rhs_r, ratio_m, ratio_r, val_m, val_r, inv_m, inv_r, rim_x, faces,
    vel_in, vout, grad, grad_in, row1, row2, sum1, sum2,
    load_sem, out_sem, a2a_send, a2a_recv, small_send, small_recv, halo_send, halo_recv,
    vel_send, vel_recv, grad_send, grad_recv, s1_send, s1_recv, s2_send, s2_recv, token,
):
    M = lax.axis_index("map")
    L = lax.axis_index("layer")
    z, y_lo, core = place(M)
    x = lax.div(L, 2)
    y = lax.rem(L, 2) * 4 + y_lo
    bm, bl = block_of(x, y, z, core)
    below = owner_of(lax.rem(bm + BLOCKS - 1, BLOCKS), bl)
    above = owner_of(lax.rem(bm + 1, BLOCKS), bl)
    owners = [owner_of(M, jnp.int32(l)) for l in range(SLOTS)]
    holders = [(bm, jnp.int32(l)) for l in range(SLOTS)]

    def peer_z(j):
        return device_at(x, y, lax.div(j, 2), lax.rem(j, 2))

    def peer_xy(j):
        return device_at(lax.div(j, 8), lax.rem(j, 8), z, core)

    stages = (
        (z * 2 + core, peer_z, row1, sum1, s1_send, s1_recv),
        (x * 8 + y, peer_xy, row2, sum2, s2_send, s2_recv),
    )

    def along_z(far):
        return device_at(x, y, lax.rem(far, 16), core)

    partners = owners + holders + [below, above, along_z(z + 1), along_z(z + 15)]
    barrier = pltpu.get_barrier_semaphore()
    for partner in partners:
        pl.semaphore_signal(barrier, inc=1, device_id=partner, device_id_type=MESH)

    loads = [
        pltpu.make_async_copy(src, dst, load_sem.at[i])
        for i, (src, dst) in enumerate(
            ((vel_hbm, vin.at[8:264]), (drv_hbm, drv), (obs_hbm, obs), (logf_hbm, logf), (mask_hbm, mask))
        )
    ]
    for load in loads:
        load.start()
    for load in loads[1:]:
        load.wait()
    small[0:8, :] = drv[...]
    small[8:16, :] = obs[...]
    small[16:20, :] = jnp.exp(logf[...]) * (mask[...] == 1).astype(f32)
    small[20:24, :] = (mask[...] != 0).astype(f32)
    loads[0].wait()

    lane2 = lax.broadcasted_iota(jnp.int32, (2, 128), 1)
    lane8 = lax.broadcasted_iota(jnp.int32, (8, 128), 1)
    row8 = lax.broadcasted_iota(jnp.int32, (8, 128), 0)
    zero = jnp.zeros((8, 128), f32)

    def turn(v):
        return pltpu.roll(v, 64, 1)

    def pack(right_a, left_a, right_b, left_b):
        low = jnp.where(lane8 < 32, right_a, turn(left_a))
        return jnp.where(lane8 < 64, low, jnp.where(lane8 < 96, turn(right_b), left_b))

    for c in range(2):
        for kk in range(4):
            for s in range(4):
                stage[pl.ds(kk * 8 + c * 4 + s, 8, stride=SLAB), :] = vin[pl.ds(8 + (c * 4 + kk) * 32 + s, 8, stride=4), :]
        for q in range(2):
            for r in range(2):
                sides = []
                for kk in (2 * q, 2 * q + 1):
                    first = 8 + (c * 4 + kk) * 32 + r
                    sides.append(jnp.where(row8 < SLOTS - 1, vin[pl.ds(first + 4, 8, stride=4), :], 0.0))
                    sides.append(jnp.where(row8 > 0, vin[pl.ds(first - 2, 8, stride=4), :], 0.0))
                stage[pl.ds(32 + q * 4 + c * 2 + r, 8, stride=SLAB), :] = pack(*sides)

    pl.semaphore_wait(barrier, len(partners))

    def give_tokens(level):
        for way, far in ((0, z + (1 << level)), (1, z + 16 - (1 << level))):
            pl.semaphore_signal(token.at[level * 2 + way], inc=1, device_id=along_z(far), device_id_type=MESH)

    def take_tokens(level):
        for way in range(2):
            pl.semaphore_wait(token.at[level * 2 + way], 1)

    give_tokens(0)
    sends = []

    def remote(src, dst, send_sem, recv_sem, device):
        copy = pltpu.make_async_remote_copy(
            src_ref=src, dst_ref=dst, send_sem=send_sem, recv_sem=recv_sem, device_id=device, device_id_type=MESH
        )
        copy.start()
        sends.append(copy)

    def arrived(ref, sem):
        pltpu.make_async_copy(ref, ref, sem).wait()

    rows = pl.ds(pl.multiple_of(L * SLAB, 8), SLAB)
    for l in range(SLOTS):
        remote(stage.at[l * SLAB:l * SLAB + SLAB], w0.at[rows], a2a_send.at[l], a2a_recv.at[L], owners[l])
    for side in range(3):
        target = owner_of(M, lax.rem(L + SLOTS + 1 - side, SLOTS))
        remote(small, small_in.at[side], small_send.at[side], small_recv.at[side], target)

    take_tokens(0)
    give_tokens(1)
    for l in range(SLOTS):
        rows = pl.ds(l * SLAB, SLAB)
        arrived(w0.at[rows], a2a_recv.at[l])
        for i, (device, land) in enumerate(((below, up0), (above, dn0))):
            pltpu.make_async_remote_copy(
                src_ref=w0.at[rows], dst_ref=land.at[rows], send_sem=halo_send.at[0, i],
                recv_sem=halo_recv.at[0, i], device_id=device, device_id_type=MESH,
            ).start()

    take_tokens(1)
    give_tokens(2)
    for side in range(3):
        arrived(small_in.at[side], small_recv.at[side])
    has_left = (bl > 0).astype(f32)
    has_right = (bl < SLOTS - 1).astype(f32)
    has_below = (bm > 0).astype(f32)
    has_above = (bm < BLOCKS - 1).astype(f32)

    def double(rows):
        return jnp.concatenate([rows, rows], 0)

    def rim_rows(start, comps):
        parts = []
        for c in range(comps):
            at = start + 4 * c
            parts.append(jnp.where(lane2 < 64, small_in[2, at:at + 2, :] * has_right, small_in[0, at + 2:at + 4, :] * has_left))
        if comps == 1:
            parts = parts * 2
        return double(jnp.concatenate(parts, 0))

    drive = (small_in[1, 0:8, :], rim_rows(0, 2))
    seen = (small_in[1, 8:16, :], rim_rows(8, 2))
    bed = (double(small_in[1, 16:20, :]), rim_rows(16, 1))
    ice = (double(small_in[1, 20:24, :]) > 0.5, rim_rows(20, 1) > 0.5)

    def ahead(tiles):
        turned = [pltpu.roll(t, 127, 1) for t in tiles]
        return [jnp.where(lane8 == 127, turned[(i + 1) % 3], turned[i]) for i in range(3)]

    def behind(tiles):
        turned = [pltpu.roll(t, 1, 1) for t in tiles]
        return [jnp.where(lane8 == 0, turned[(i + 2) % 3], turned[i]) for i in range(3)]

    def load_tiles(slab, c, r, kk, packed):
        tiles = [slab[pl.ds(kk * 8 + c * 4 + t * 2 + r, 8, stride=SLAB), :] for t in range(2)]
        return tiles + [packed[kk % 2]]

    def unpack(slab, c, r, q):
        v = slab[pl.ds(32 + q * 4 + c * 2 + r, 8, stride=SLAB), :]
        turned = turn(v)
        return jnp.where(lane8 < 64, v, turned), jnp.where(lane8 < 64, turned, v)

    def store_tile(main, rim, kk, c, t, r, value):
        if t < 2:
            main[pl.ds(kk * 8 + c * 4 + t * 2 + r, 8, stride=32), :] = value
        else:
            rim[pl.ds(kk * 8 + c * 2 + r, 8, stride=32), :] = value

    def scaled(tiles, factor):
        return [t * factor for t in tiles]

    def forward_terms(own, low, high):
        for q in range(2):
            rims = [[unpack(slab, c, r, q) for slab in (low, own, high) for r in range(2)] for c in range(2)]
            for kk in (2 * q, 2 * q + 1):
                group(own, low, high, kk, rims)

    def group(own, low, high, kk, rims):
        w = []
        for c in range(2):
            rows = [scaled(load_tiles(low, c, r, kk, rims[c][r]), has_below) for r in range(2)]
            rows += [load_tiles(own, c, r, kk, rims[c][2 + r]) for r in range(2)]
            rows += [scaled(load_tiles(high, c, r, kk, rims[c][4 + r]), has_above) for r in range(2)]
            w.append(rows)
        right = [[ahead(w[c][r]) for r in range(1, 5)] for c in range(2)]
        left = [[behind(w[c][r]) for r in range(1, 5)] for c in range(2)]
        eta = []
        for r in range(4):
            tiles = []
            for t in range(3):
                u_x = (w[0][r + 2][t] - w[0][r][t]) * 0.5
                v_x = (w[1][r + 2][t] - w[1][r][t]) * 0.5
                u_y = (right[0][r][t] - left[0][r][t]) * 0.5
                v_y = (right[1][r][t] - left[1][r][t]) * 0.5
                shear = u_y + v_x
                rate = u_x * u_x + v_y * v_y + u_x * v_y + 0.25 * shear * shear
                tiles.append(jnp.exp(jnp.log(strain_floor + rate) * (-1.0 / 3.0)))
            eta.append(tiles)
        for r in range(2):
            eta_right, eta_left = ahead(eta[r + 1]), behind(eta[r + 1])
            for t in range(3):
                centre = eta[r + 1][t]
                east = 0.5 * (centre + eta[r + 2][t])
                west = 0.5 * (centre + eta[r][t])
                north = 0.5 * (centre + eta_right[t])
                south = 0.5 * (centre + eta_left[t])
                along, across = east + west, north + south
                if t < 2:
                    for i, face in enumerate((east, west, north, south)):
                        faces[kk, (r * 2 + t) * 4 + i] = face
                u, v = w
                sum_u = (
                    4.0 * (east * u[r + 3][t] + west * u[r + 1][t])
                    + north * right[0][r + 1][t] + south * left[0][r + 1][t]
                )
                sum_v = (
                    east * v[r + 3][t] + west * v[r + 1][t]
                    + 4.0 * (north * right[1][r + 1][t] + south * left[1][r + 1][t])
                )
                store_tile(eta_m, eta_r, kk, 0, t, r, centre)
                store_tile(eta_m, eta_r, kk, 1, t, r, centre)
                store_tile(diag_m, diag_r, kk, 0, t, r, 4.0 * along + across)
                store_tile(diag_m, diag_r, kk, 1, t, r, along + 4.0 * across)
                store_tile(rhs_m, rhs_r, kk, 0, t, r, sum_u)
                store_tile(rhs_m, rhs_r, kk, 1, t, r, sum_v)

    pairs = (
        (eta_m, diag_m, rhs_m, ratio_m, val_m, inv_m),
        (eta_r, diag_r, rhs_r, ratio_r, val_r, inv_r),
    )

    def at(k):
        return pl.ds(pl.multiple_of(k * 8, 8), 8)

    def solve(out):
        def eliminate(k, carry, last=False):
            new = []
            for part in range(2):
                eta, diag, rhs, ratio, val, inv = pairs[part]
                lower, ratio_prev, val_prev, pad = carry[part]
                upper = zero if last else 1024.0 * (eta[at(k), :] + eta[at(k + 1), :])
                inverse = 1.0 / (((lower + upper + pad) + diag[at(k), :]) + lower * ratio_prev)
                ratio_now = -upper * inverse
                val_now = (drive[part] + rhs[at(k), :] + lower * val_prev) * inverse
                ratio[at(k), :] = ratio_now
                val[at(k), :] = val_now
                inv[at(k), :] = inverse
                new.append((upper, ratio_now, val_now, zero))
            return tuple(new)

        carry = tuple((zero, zero, zero, bed[part]) for part in range(2))
        carry = lax.fori_loop(0, LAYERS - 1, eliminate, carry)
        eliminate(LAYERS - 1, carry, last=True)

        def substitute(i, following):
            slot = SLOTS - 1 - i
            for kk in reversed(range(4)):
                k = slot * 4 + kk
                new = []
                for part, (to, where) in enumerate(((out, pl.ds(pl.multiple_of(slot * SLAB + kk * 8, 8), 8)), (rim_x, at(k)))):
                    ratio, val = pairs[part][3], pairs[part][4]
                    now = val[at(k), :] - ratio[at(k), :] * following[part]
                    to[where, :] = jnp.where(ice[part], now, 0.0)
                    new.append(now)
                following = tuple(new)
            return following

        lax.fori_loop(0, SLOTS, substitute, (zero, zero))

    def pack_rims(out):
        for q in range(2):
            for s in range(4):
                a = rim_x[pl.ds(2 * q * 8 + s, 8, stride=32), :]
                b = rim_x[pl.ds((2 * q + 1) * 8 + s, 8, stride=32), :]
                out[pl.ds(32 + q * 4 + s, 8, stride=SLAB), :] = pack(a, a, b, b)

    for i, land in enumerate((up0, dn0)):
        arrived(land, halo_recv.at[0, i])
    forward_terms(w0, dn0, up0)
    solve(w1)
    pack_rims(w1)
    for i, (device, land) in enumerate(((below, up1), (above, dn1))):
        remote(w1, land, halo_send.at[1, i], halo_recv.at[1, i], device)

    for i, land in enumerate((up1, dn1)):
        arrived(land, halo_recv.at[1, i])
    forward_terms(w1, dn1, up1)
    solve(w2)
    take_tokens(2)

    top = LAYERS - 1
    last = (SLOTS - 1) * SLAB + 24
    tops = (w2[last:last + 8, :], rim_x[at(top), :])
    mismatch = [jnp.where(ice[part], tops[part] - seen[part], 0.0) for part in range(2)]
    source = [float(LAYERS) * mismatch[part] for part in range(2)]
    starts = tuple(source[part] * pairs[part][5][at(top), :] for part in range(2))
    adjoints = (am, rim_x)
    for part in range(2):
        adjoints[part][at(top), :] = jnp.where(ice[part], starts[part], 0.0)

    def substitute_first(i, following):
        k = LAYERS - 2 - i
        new = []
        for part in range(2):
            now = -pairs[part][3][at(k), :] * following[part]
            adjoints[part][at(k), :] = jnp.where(ice[part], now, 0.0)
            new.append(now)
        return tuple(new)

    lax.fori_loop(0, LAYERS - 1, substitute_first, starts)
    for r, (edge, land, device) in enumerate(((alow, aup, below), (ahigh, adn, above))):
        for s in range(4):
            for j in range(GROUPS):
                edge[pl.ds(j * 4 + s, 8, stride=16), :] = am[pl.ds(j * 8 + s * 2 + r, 8, stride=32), :]
        remote(edge, land, halo_send.at[2, r], halo_recv.at[2, r], device)

    arrived(aup, halo_recv.at[2, 0])
    arrived(adn, halo_recv.at[2, 1])

    for kk in range(4):
        for c in range(2):
            rows = [[am[pl.ds(kk * 8 + c * 4 + t * 2 + r, 8, stride=32), :] for t in range(2)] for r in range(2)]
            for r in range(2):
                rows[r].append(rim_x[pl.ds(kk * 8 + c * 2 + r, 8, stride=32), :])
            for r in range(2):
                right, left = ahead(rows[r]), behind(rows[r])
                for t in range(2):
                    if r == 0:
                        low = adn[pl.ds(kk * 4 + c * 2 + t, 8, stride=16), :] * has_below
                        high = rows[1][t]
                    else:
                        low = rows[0][t]
                        high = aup[pl.ds(kk * 4 + c * 2 + t, 8, stride=16), :] * has_above
                    east, west, north, south = [faces[kk, (r * 2 + t) * 4 + i] for i in range(4)]
                    along = east * high + west * low
                    across = north * right[t] + south * left[t]
                    value = 4.0 * along + across if c == 0 else along + 4.0 * across
                    rhs_m[pl.ds(kk * 8 + c * 4 + t * 2 + r, 8, stride=32), :] = value
    rhs_m[at(top), :] = rhs_m[at(top), :] + source[0]

    def eliminate_second(k, prev):
        lower = 1024.0 * (eta_m[at(k - 1), :] + eta_m[at(k), :])
        now = (rhs_m[at(k), :] + lower * prev) * inv_m[at(k), :]
        val_m[at(k), :] = now
        return now

    first = rhs_m[0:8, :] * inv_m[0:8, :]
    val_m[0:8, :] = first
    lax.fori_loop(1, LAYERS, eliminate_second, first)

    def substitute_second(i, following):
        k = LAYERS - 1 - i
        return val_m[at(k), :] - ratio_m[at(k), :] * following

    bottom = jnp.where(ice[0], lax.fori_loop(0, LAYERS, substitute_second, zero), 0.0)

    product = w2[0:8, :] * bottom
    gradient = -bed[0][0:4, :] * (product[0:4, :] + product[4:8, :])
    grad[...] = gradient
    remote(grad, grad_in, grad_send, grad_recv, (bm, bl))

    lane1 = lax.broadcasted_iota(jnp.int32, (1, 128), 1)
    grad_row = jnp.sum(gradient * gradient, axis=0, keepdims=True)
    fit_row = jnp.sum(0.5 * mismatch[0] * mismatch[0], axis=0, keepdims=True)
    grad_row = grad_row + pltpu.roll(grad_row, 64, 1)
    fit_row = fit_row + pltpu.roll(fit_row, 64, 1)
    row = jnp.where(lane1 < 64, grad_row, fit_row)
    for number, (me, peer, row_ref, sum_ref, send_sem, recv_sem) in enumerate(stages):
        count = 32
        row_ref[...] = row
        sum_ref[me] = row
        order = sorted(range(1, count), key=lambda i: -min(i, count - i)) if number == 0 else reversed(range(1, count))
        for i in order:
            other = lax.rem(me + i, count)
            remote(row_ref, sum_ref.at[me], send_sem.at[i], recv_sem.at[me], peer(other))
        if number == 0:
            for l in range(SLOTS):
                remote(
                    w2.at[l * SLAB:l * SLAB + 32], vel_in.at[pl.ds(pl.multiple_of(bl * 32, 32), 32)],
                    vel_send.at[l], vel_recv.at[bl], holders[l],
                )
        else:
            for l in range(SLOTS):
                arrived(vel_in.at[l * 32:l * 32 + 32], vel_recv.at[l])
            for c in range(2):
                for kk in range(4):
                    for s in range(4):
                        piece = vel_in[pl.ds(kk * 8 + c * 4 + s, 8, stride=32), :]
                        vout[pl.ds((c * 4 + kk) * 32 + s, 8, stride=4), :] = piece
            store = pltpu.make_async_copy(vout, out_hbm, out_sem)
            store.start()
        for i in range(1, count):
            other = lax.rem(me + i, count)
            arrived(sum_ref.at[other], recv_sem.at[other])
        parts = [sum_ref[i] for i in range(count)]
        while len(parts) > 1:
            parts = [parts[i] + parts[i + 1] for i in range(0, len(parts), 2)]
        row = parts[0]

    grad_total = jnp.sum(jnp.where(lane1 < 64, row, 0.0))
    fit_total = jnp.sum(jnp.where(lane1 < 64, 0.0, row))
    misfit_out[0, 0] = fit_total / COLUMNS
    arrived(grad_in, grad_recv)
    scale = jnp.sqrt(jnp.full((4, 128), grad_total, f32) / COLUMNS + 1e-06)
    fric_out[...] = logf[...] - step_size * grad_in[...] / scale

    for copy in sends:
        copy.wait_send()
    for i in range(2):
        arrived(w0, halo_send.at[0, i])
    store.wait()


def on_device(velocity_init, driving, observed, log_friction, ice_mask):
    vel = velocity_init.reshape(2, 4, 2, 16, 128).transpose(0, 1, 3, 2, 4).reshape(256, 128)

    def tiles(a, lead):
        b = a.reshape(lead, 2, 2, 128).transpose(0, 2, 1, 3)
        return b.reshape(lead * 4, 128)

    full, half, slab = (256, 128), (128, 128), (SLOTS * SLAB, 128)
    vm = lambda shape: pltpu.VMEM(shape, f32)
    dma = pltpu.SemaphoreType.DMA
    scratch = [vm((272, 128)), vm((8, 128)), vm((8, 128)), vm((4, 128)), pltpu.VMEM((4, 128), jnp.int32)]
    scratch += [vm(slab), vm((24, 128)), vm((3, 24, 128))]
    scratch += [vm(slab)] * 7 + [vm(full)] + [vm(half)] * 4
    scratch += [vm(full)] * 13 + [vm((GROUPS, 16, 8, 128))]
    scratch += [vm(full), vm(full), vm((4, 128)), vm((4, 128))]
    scratch += [vm((1, 128))] * 2 + [vm((32, 1, 128))] * 2
    scratch += [dma((5,)), dma, dma((8,)), dma((8,)), dma((3,)), dma((3,)), dma((3, 2)), dma((3, 2))]
    scratch += [dma((8,)), dma((8,)), dma, dma] + [dma((32,))] * 4 + [pltpu.SemaphoreType.REGULAR((6,))]
    anywhere = pl.BlockSpec(memory_space=pl.ANY)
    out, fric, misfit = pl.pallas_call(
        kernel,
        out_shape=(
            jax.ShapeDtypeStruct(full, f32),
            jax.ShapeDtypeStruct((4, 128), f32),
            jax.ShapeDtypeStruct((1, 1), f32),
        ),
        in_specs=[anywhere] * 5,
        out_specs=(
            anywhere,
            pl.BlockSpec(memory_space=pltpu.VMEM),
            pl.BlockSpec(memory_space=pltpu.SMEM),
        ),
        scratch_shapes=scratch,
        compiler_params=pltpu.CompilerParams(collective_id=0, has_side_effects=True),
    )(vel, tiles(driving, 2), tiles(observed, 2), tiles(log_friction, 1), tiles(ice_mask, 1))
    velocity = out.reshape(2, 4, 16, 2, 128).transpose(0, 1, 3, 2, 4).reshape(2, 4, 2, 2048)
    fric = fric.reshape(2, 2, 128).transpose(1, 0, 2).reshape(2, 256)
    return velocity, fric, misfit.reshape(())


def solution(mesh):
    in_specs = (
        P(None, "layer", "map", None),
        P(None, "map", "layer"),
        P(None, "map", "layer"),
        P("map", "layer"),
        P("map", "layer"),
    )
    out_specs = (P(None, "layer", "map", None), P("map", "layer"), P())
    return jax.shard_map(on_device, mesh=mesh, in_specs=in_specs, out_specs=out_specs, check_vma=False)
```

time: 69.6 us -> 64.6 us (0.928)
  Pallas kernels: 64.2 us -> 59.8 us
    pallas_call x1, Pallas kernels: 64.2 us -> 59.8 us  [on_device(): pl.pallas_call(kernel, out_shape=(jax.ShapeDtypeStruct(full, f32), jax.Sh...]
where the time goes in v2:
time: 64.6 us; the launch traced here: 64.4 us
  Pallas kernels  59.8 us (93%)
  between operations  2.41 us (4%)
  local copies, waits for them, and re-layouts  2.15 us (3%)
    pallas_call x1, Pallas kernels, on_device(): pl.pallas_call(kernel, out_shape=(jax.ShapeDtypeStruct(full, f32), jax.Sh...  59.8 us
    unnamed x4, local copies, waits for them, and re-layouts  2.15 us

profile of v2, /device:TPU:1, one launch (start us, length us, event | category | flops | bytes accessed | tf_op | source)
XLA Modules:
  0.0 64.4 jit_solution(6869776027653307644)
XLA Ops:
  0.6 59.8 %shard_map.76 = (f32[256,128]{1,0:T(8,128)}, f32[4,128]{1,0:T(4,128)}, f32[1,1]{1,0:T(1,128)}) custom-call(f32[256,128]{1,0:T(8,128)} %bitcast.36, f32[8,128]{1,0:T(8,128)} %bitcast.38, f32[8,128]{1,0:T(8,128)} %bitcast.39, f32[4,128]{1,0:T(4,128)} %bitcast.40, s32[4,128]{1,0:T(4,128)} %bitcast.41), custom_call_target="tpu_custom_call" | custom-call | tf_op jit(solution)/shard_map/pallas_call | solution.py:476
  60.5 0.0 copy-start
  60.5 1.6 %copy.18 = f32[2,4,2,2048]{3,2,1,0:T(2,128)} copy(f32[2,4,2,2048]{3,2,1,0:T(2,128)} %bitcast.37) | data formatting | bytes 262144
  62.0 0.0 copy-done
  62.0 0.6 copy.19
Async XLA Ops:
  60.5 1.6 %copy-start = (f32[4,128]{1,0:T(4,128)S(1)}, f32[4,128]{1,0:T(4,128)}, u32[]{:S(2)}) copy-start(f32[4,128]{1,0:T(4,128)} %get-tuple-element.7) | copy-start | bytes 6148

commit v3 on v2

--- a/solution.py
+++ b/solution.py
@@ -40,14 +40,23 @@
 
 def kernel(
     vel_hbm, drv_hbm, obs_hbm, logf_hbm, mask_hbm,
-    out_hbm, fric_out, misfit_out,
+    vout, fric_out, misfit_out,
     vin, drv, obs, logf, mask, stage, small, small_in,
     w0, w1, w2, dn0, up0, dn1, up1, am, adn, aup, alow, ahigh,
     eta_m, eta_r, diag_m, diag_r, rhs_m, rhs_r, ratio_m, ratio_r, val_m, val_r, inv_m, inv_r, rim_x, faces,
-    vel_in, vout, grad, grad_in, row1, row2, sum1, sum2,
-    load_sem, out_sem, a2a_send, a2a_recv, small_send, small_recv, halo_send, halo_recv,
+    vel_in, grad, grad_in, row1, row2, sum1, sum2,
+    load_sem, a2a_send, a2a_recv, small_send, small_recv, halo_send, halo_recv,
     vel_send, vel_recv, grad_send, grad_recv, s1_send, s1_recv, s2_send, s2_recv, token,
 ):
+    loads = [
+        pltpu.make_async_copy(src, dst, load_sem.at[i])
+        for i, (src, dst) in enumerate(
+            ((vel_hbm, vin.at[8:264]), (drv_hbm, drv), (obs_hbm, obs), (logf_hbm, logf), (mask_hbm, mask))
+        )
+    ]
+    for load in loads:
+        load.start()
+
     M = lax.axis_index("map")
     L = lax.axis_index("layer")
     z, y_lo, core = place(M)
@@ -65,9 +74,14 @@
     def peer_xy(j):
         return device_at(lax.div(j, 8), lax.rem(j, 8), z, core)
 
+    ring_z = sorted(((dz, dc) for dz in range(16) for dc in range(2)), key=lambda d: -min(d[0], 16 - d[0]) - d[1] / 2)[:-1]
+    ring_xy = sorted(((dx, dy) for dx in range(4) for dy in range(8)), key=lambda d: -min(d[0], 4 - d[0]) - min(d[1], 8 - d[1]))[:-1]
+    zs = [lax.rem(z + dz, 16) for dz in range(16)]
+    xs = [lax.rem(x + dx, 4) for dx in range(4)]
+    ys = [lax.rem(y + dy, 8) for dy in range(8)]
     stages = (
-        (z * 2 + core, peer_z, row1, sum1, s1_send, s1_recv),
-        (x * 8 + y, peer_xy, row2, sum2, s2_send, s2_recv),
+        (z * 2 + core, [zs[dz] * 2 + (1 - core if dc else core) for dz, dc in ring_z], peer_z, row1, sum1, s1_send, s1_recv),
+        (x * 8 + y, [xs[dx] * 8 + ys[dy] for dx, dy in ring_xy], peer_xy, row2, sum2, s2_send, s2_recv),
     )
 
     def along_z(far):
@@ -78,14 +92,6 @@
     for partner in partners:
         pl.semaphore_signal(barrier, inc=1, device_id=partner, device_id_type=MESH)
 
-    loads = [
-        pltpu.make_async_copy(src, dst, load_sem.at[i])
-        for i, (src, dst) in enumerate(
-            ((vel_hbm, vin.at[8:264]), (drv_hbm, drv), (obs_hbm, obs), (logf_hbm, logf), (mask_hbm, mask))
-        )
-    ]
-    for load in loads:
-        load.start()
     for load in loads[1:]:
         load.wait()
     small[0:8, :] = drv[...]
@@ -139,6 +145,18 @@
         copy.start()
         sends.append(copy)
 
+    bulk = []
+
+    def pieces(src, dst, count, index, device):
+        size = src.shape[0] // count
+        for i in reversed(range(count)):
+            rows = pl.ds(i * size, size)
+            pltpu.make_async_remote_copy(
+                src_ref=src.at[rows], dst_ref=dst.at[rows], send_sem=halo_send.at[index],
+                recv_sem=halo_recv.at[index], device_id=device, device_id_type=MESH,
+            ).start()
+        bulk.append((src, halo_send.at[index]))
+
     def arrived(ref, sem):
         pltpu.make_async_copy(ref, ref, sem).wait()
 
@@ -205,9 +223,9 @@
 
     def store_tile(main, rim, kk, c, t, r, value):
         if t < 2:
-            main[pl.ds(kk * 8 + c * 4 + t * 2 + r, 8, stride=32), :] = value
+            main[pl.ds(kk * 8 + c * 4 + t * 2 + r, 8, stride=SLAB), :] = value
         else:
-            rim[pl.ds(kk * 8 + c * 2 + r, 8, stride=32), :] = value
+            rim[pl.ds(kk * 8 + c * 2 + r, 8, stride=SLAB), :] = value
 
     def scaled(tiles, factor):
         return [t * factor for t in tiles]
@@ -272,38 +290,44 @@
         (eta_r, diag_r, rhs_r, ratio_r, val_r, inv_r),
     )
 
-    def at(k):
-        return pl.ds(pl.multiple_of(k * 8, 8), 8)
+    def at(slot, kk):
+        return pl.ds(pl.multiple_of(slot * SLAB + kk * 8, 8), 8)
 
     def solve(out):
-        def eliminate(k, carry, last=False):
-            new = []
-            for part in range(2):
-                eta, diag, rhs, ratio, val, inv = pairs[part]
-                lower, ratio_prev, val_prev, pad = carry[part]
-                upper = zero if last else 1024.0 * (eta[at(k), :] + eta[at(k + 1), :])
-                inverse = 1.0 / (((lower + upper + pad) + diag[at(k), :]) + lower * ratio_prev)
-                ratio_now = -upper * inverse
-                val_now = (drive[part] + rhs[at(k), :] + lower * val_prev) * inverse
-                ratio[at(k), :] = ratio_now
-                val[at(k), :] = val_now
-                inv[at(k), :] = inverse
-                new.append((upper, ratio_now, val_now, zero))
-            return tuple(new)
+        def eliminate(slot, carry, last=False):
+            for kk in range(4):
+                new = []
+                for part in range(2):
+                    eta, diag, rhs, ratio, val, inv = pairs[part]
+                    lower, ratio_prev, val_prev, pad = carry[part]
+                    k = at(slot, kk)
+                    if last and kk == 3:
+                        upper = zero
+                    else:
+                        upper = 1024.0 * (eta[k, :] + eta[at(slot, kk + 1) if kk < 3 else at(slot + 1, 0), :])
+                    inverse = 1.0 / (((lower + upper + pad) + diag[k, :]) + lower * ratio_prev)
+                    ratio_now = -upper * inverse
+                    val_now = (drive[part] + rhs[k, :] + lower * val_prev) * inverse
+                    ratio[k, :] = ratio_now
+                    val[k, :] = val_now
+                    inv[k, :] = inverse
+                    new.append((upper, ratio_now, val_now, zero))
+                carry = tuple(new)
+            return carry
 
         carry = tuple((zero, zero, zero, bed[part]) for part in range(2))
-        carry = lax.fori_loop(0, LAYERS - 1, eliminate, carry)
-        eliminate(LAYERS - 1, carry, last=True)
+        carry = lax.fori_loop(0, SLOTS - 1, eliminate, carry)
+        eliminate(SLOTS - 1, carry, last=True)
 
         def substitute(i, following):
             slot = SLOTS - 1 - i
             for kk in reversed(range(4)):
-                k = slot * 4 + kk
+                k = at(slot, kk)
                 new = []
-                for part, (to, where) in enumerate(((out, pl.ds(pl.multiple_of(slot * SLAB + kk * 8, 8), 8)), (rim_x, at(k)))):
+                for part, to in enumerate((out, rim_x)):
                     ratio, val = pairs[part][3], pairs[part][4]
-                    now = val[at(k), :] - ratio[at(k), :] * following[part]
-                    to[where, :] = jnp.where(ice[part], now, 0.0)
+                    now = val[k, :] - ratio[k, :] * following[part]
+                    to[k, :] = jnp.where(ice[part], now, 0.0)
                     new.append(now)
                 following = tuple(new)
             return following
@@ -313,8 +337,8 @@
     def pack_rims(out):
         for q in range(2):
             for s in range(4):
-                a = rim_x[pl.ds(2 * q * 8 + s, 8, stride=32), :]
-                b = rim_x[pl.ds((2 * q + 1) * 8 + s, 8, stride=32), :]
+                a = rim_x[pl.ds(2 * q * 8 + s, 8, stride=SLAB), :]
+                b = rim_x[pl.ds((2 * q + 1) * 8 + s, 8, stride=SLAB), :]
                 out[pl.ds(32 + q * 4 + s, 8, stride=SLAB), :] = pack(a, a, b, b)
 
     for i, land in enumerate((up0, dn0)):
@@ -323,7 +347,7 @@
     solve(w1)
     pack_rims(w1)
     for i, (device, land) in enumerate(((below, up1), (above, dn1))):
-        remote(w1, land, halo_send.at[1, i], halo_recv.at[1, i], device)
+        pieces(w1, land, SLOTS, (1, i), device)
 
     for i, land in enumerate((up1, dn1)):
         arrived(land, halo_recv.at[1, i])
@@ -331,71 +355,78 @@
     solve(w2)
     take_tokens(2)
 
-    top = LAYERS - 1
-    last = (SLOTS - 1) * SLAB + 24
-    tops = (w2[last:last + 8, :], rim_x[at(top), :])
+    top = pl.ds((SLOTS - 1) * SLAB + 24, 8)
+    tops = (w2[top, :], rim_x[top, :])
     mismatch = [jnp.where(ice[part], tops[part] - seen[part], 0.0) for part in range(2)]
     source = [float(LAYERS) * mismatch[part] for part in range(2)]
-    starts = tuple(source[part] * pairs[part][5][at(top), :] for part in range(2))
+    starts = tuple(source[part] * pairs[part][5][top, :] for part in range(2))
     adjoints = (am, rim_x)
     for part in range(2):
-        adjoints[part][at(top), :] = jnp.where(ice[part], starts[part], 0.0)
-
-    def substitute_first(i, following):
-        k = LAYERS - 2 - i
-        new = []
-        for part in range(2):
-            now = -pairs[part][3][at(k), :] * following[part]
-            adjoints[part][at(k), :] = jnp.where(ice[part], now, 0.0)
-            new.append(now)
-        return tuple(new)
-
-    lax.fori_loop(0, LAYERS - 1, substitute_first, starts)
+        adjoints[part][top, :] = jnp.where(ice[part], starts[part], 0.0)
+
+    def substitute_first(slot, following, steps=range(4)):
+        for kk in reversed(steps):
+            k = at(slot, kk)
+            new = []
+            for part in range(2):
+                now = -pairs[part][3][k, :] * following[part]
+                adjoints[part][k, :] = jnp.where(ice[part], now, 0.0)
+                new.append(now)
+            following = tuple(new)
+        return following
+
+    following = substitute_first(SLOTS - 1, starts, range(3))
+    lax.fori_loop(1, SLOTS, lambda i, carry: substitute_first(SLOTS - 1 - i, carry), following)
     for r, (edge, land, device) in enumerate(((alow, aup, below), (ahigh, adn, above))):
         for s in range(4):
             for j in range(GROUPS):
-                edge[pl.ds(j * 4 + s, 8, stride=16), :] = am[pl.ds(j * 8 + s * 2 + r, 8, stride=32), :]
-        remote(edge, land, halo_send.at[2, r], halo_recv.at[2, r], device)
+                edge[pl.ds(j * 32 + s, 8, stride=4), :] = am[pl.ds(j * 8 + s * 2 + r, 8, stride=SLAB), :]
+        pieces(edge, land, 4, (2, r), device)
 
     arrived(aup, halo_recv.at[2, 0])
     arrived(adn, halo_recv.at[2, 1])
 
     for kk in range(4):
         for c in range(2):
-            rows = [[am[pl.ds(kk * 8 + c * 4 + t * 2 + r, 8, stride=32), :] for t in range(2)] for r in range(2)]
+            rows = [[am[pl.ds(kk * 8 + c * 4 + t * 2 + r, 8, stride=SLAB), :] for t in range(2)] for r in range(2)]
             for r in range(2):
-                rows[r].append(rim_x[pl.ds(kk * 8 + c * 2 + r, 8, stride=32), :])
+                rows[r].append(rim_x[pl.ds(kk * 8 + c * 2 + r, 8, stride=SLAB), :])
             for r in range(2):
                 right, left = ahead(rows[r]), behind(rows[r])
                 for t in range(2):
                     if r == 0:
-                        low = adn[pl.ds(kk * 4 + c * 2 + t, 8, stride=16), :] * has_below
+                        low = adn[pl.ds(kk * 32 + c * 2 + t, 8, stride=4), :] * has_below
                         high = rows[1][t]
                     else:
                         low = rows[0][t]
-                        high = aup[pl.ds(kk * 4 + c * 2 + t, 8, stride=16), :] * has_above
+                        high = aup[pl.ds(kk * 32 + c * 2 + t, 8, stride=4), :] * has_above
                     east, west, north, south = [faces[kk, (r * 2 + t) * 4 + i] for i in range(4)]
                     along = east * high + west * low
                     across = north * right[t] + south * left[t]
                     value = 4.0 * along + across if c == 0 else along + 4.0 * across
-                    rhs_m[pl.ds(kk * 8 + c * 4 + t * 2 + r, 8, stride=32), :] = value
-    rhs_m[at(top), :] = rhs_m[at(top), :] + source[0]
-
-    def eliminate_second(k, prev):
-        lower = 1024.0 * (eta_m[at(k - 1), :] + eta_m[at(k), :])
-        now = (rhs_m[at(k), :] + lower * prev) * inv_m[at(k), :]
-        val_m[at(k), :] = now
-        return now
+                    rhs_m[pl.ds(kk * 8 + c * 4 + t * 2 + r, 8, stride=SLAB), :] = value
+    rhs_m[top, :] = rhs_m[top, :] + source[0]
+
+    def eliminate_second(slot, prev, steps=range(4)):
+        for kk in steps:
+            k, under = at(slot, kk), at(slot, kk - 1) if kk > 0 else at(slot - 1, 3)
+            lower = 1024.0 * (eta_m[under, :] + eta_m[k, :])
+            inverse = inv_m[k, :]
+            prev = rhs_m[k, :] * inverse + (lower * inverse) * prev
+            val_m[k, :] = prev
+        return prev
 
     first = rhs_m[0:8, :] * inv_m[0:8, :]
     val_m[0:8, :] = first
-    lax.fori_loop(1, LAYERS, eliminate_second, first)
+    lax.fori_loop(1, SLOTS, eliminate_second, eliminate_second(0, first, range(1, 4)))
 
     def substitute_second(i, following):
-        k = LAYERS - 1 - i
-        return val_m[at(k), :] - ratio_m[at(k), :] * following
-
-    bottom = jnp.where(ice[0], lax.fori_loop(0, LAYERS, substitute_second, zero), 0.0)
+        for kk in reversed(range(4)):
+            k = at(SLOTS - 1 - i, kk)
+            following = val_m[k, :] - ratio_m[k, :] * following
+        return following
+
+    bottom = jnp.where(ice[0], lax.fori_loop(0, SLOTS, substitute_second, zero), 0.0)
 
     product = w2[0:8, :] * bottom
     gradient = -bed[0][0:4, :] * (product[0:4, :] + product[4:8, :])
@@ -408,50 +439,55 @@
     grad_row = grad_row + pltpu.roll(grad_row, 64, 1)
     fit_row = fit_row + pltpu.roll(fit_row, 64, 1)
     row = jnp.where(lane1 < 64, grad_row, fit_row)
-    for number, (me, peer, row_ref, sum_ref, send_sem, recv_sem) in enumerate(stages):
-        count = 32
+    for number, (me, others, peer, row_ref, sum_ref, send_sem, recv_sem) in enumerate(stages):
         row_ref[...] = row
         sum_ref[me] = row
-        order = sorted(range(1, count), key=lambda i: -min(i, count - i)) if number == 0 else reversed(range(1, count))
-        for i in order:
-            other = lax.rem(me + i, count)
+        for i, other in enumerate(others):
             remote(row_ref, sum_ref.at[me], send_sem.at[i], recv_sem.at[me], peer(other))
         if number == 0:
             for l in range(SLOTS):
                 remote(
-                    w2.at[l * SLAB:l * SLAB + 32], vel_in.at[pl.ds(pl.multiple_of(bl * 32, 32), 32)],
+                    w2.at[l * SLAB:l * SLAB + 32], vel_in.at[pl.ds(pl.multiple_of(bl * SLAB, 8), 32)],
                     vel_send.at[l], vel_recv.at[bl], holders[l],
                 )
         else:
             for l in range(SLOTS):
-                arrived(vel_in.at[l * 32:l * 32 + 32], vel_recv.at[l])
+                arrived(vel_in.at[l * SLAB:l * SLAB + 32], vel_recv.at[l])
             for c in range(2):
                 for kk in range(4):
                     for s in range(4):
-                        piece = vel_in[pl.ds(kk * 8 + c * 4 + s, 8, stride=32), :]
+                        piece = vel_in[pl.ds(kk * 8 + c * 4 + s, 8, stride=SLAB), :]
                         vout[pl.ds((c * 4 + kk) * 32 + s, 8, stride=4), :] = piece
-            store = pltpu.make_async_copy(vout, out_hbm, out_sem)
-            store.start()
-        for i in range(1, count):
-            other = lax.rem(me + i, count)
+        for other in reversed(others):
             arrived(sum_ref.at[other], recv_sem.at[other])
-        parts = [sum_ref[i] for i in range(count)]
+        parts = [sum_ref[i] for i in range(32)]
         while len(parts) > 1:
             parts = [parts[i] + parts[i + 1] for i in range(0, len(parts), 2)]
         row = parts[0]
 
     grad_total = jnp.sum(jnp.where(lane1 < 64, row, 0.0))
     fit_total = jnp.sum(jnp.where(lane1 < 64, 0.0, row))
-    misfit_out[0, 0] = fit_total / COLUMNS
+    misfit_out[...] = jnp.full((1, 128), fit_total, f32) / COLUMNS
     arrived(grad_in, grad_recv)
     scale = jnp.sqrt(jnp.full((4, 128), grad_total, f32) / COLUMNS + 1e-06)
     fric_out[...] = logf[...] - step_size * grad_in[...] / scale
 
     for copy in sends:
         copy.wait_send()
-    for i in range(2):
-        arrived(w0, halo_send.at[0, i])
-    store.wait()
+    bulk += [(w0, halo_send.at[0, i]) for i in range(2)]
+    for src, sem in bulk:
+        arrived(src, sem)
+
+
+def hand_over(out, fric, misfit, out_hbm, fric_hbm, misfit_hbm, sem):
+    copies = [
+        pltpu.make_async_copy(src, dst, sem.at[i])
+        for i, (src, dst) in enumerate(((out, out_hbm), (fric, fric_hbm), (misfit, misfit_hbm)))
+    ]
+    for copy in copies:
+        copy.start()
+    for copy in copies:
+        copy.wait()
 
 
 def on_device(velocity_init, driving, observed, log_friction, ice_mask):
@@ -466,32 +502,43 @@
     dma = pltpu.SemaphoreType.DMA
     scratch = [vm((272, 128)), vm((8, 128)), vm((8, 128)), vm((4, 128)), pltpu.VMEM((4, 128), jnp.int32)]
     scratch += [vm(slab), vm((24, 128)), vm((3, 24, 128))]
-    scratch += [vm(slab)] * 7 + [vm(full)] + [vm(half)] * 4
-    scratch += [vm(full)] * 13 + [vm((GROUPS, 16, 8, 128))]
-    scratch += [vm(full), vm(full), vm((4, 128)), vm((4, 128))]
+    scratch += [vm(slab)] * 8 + [vm(half)] * 4
+    scratch += [vm(slab)] * 13 + [vm((GROUPS, 16, 8, 128))]
+    scratch += [vm(slab), vm((4, 128)), vm((4, 128))]
     scratch += [vm((1, 128))] * 2 + [vm((32, 1, 128))] * 2
-    scratch += [dma((5,)), dma, dma((8,)), dma((8,)), dma((3,)), dma((3,)), dma((3, 2)), dma((3, 2))]
+    scratch += [dma((5,)), dma((8,)), dma((8,)), dma((3,)), dma((3,)), dma((3, 2)), dma((3, 2))]
     scratch += [dma((8,)), dma((8,)), dma, dma] + [dma((32,))] * 4 + [pltpu.SemaphoreType.REGULAR((6,))]
     anywhere = pl.BlockSpec(memory_space=pl.ANY)
     out, fric, misfit = pl.pallas_call(
         kernel,
         out_shape=(
-            jax.ShapeDtypeStruct(full, f32),
-            jax.ShapeDtypeStruct((4, 128), f32),
-            jax.ShapeDtypeStruct((1, 1), f32),
+            pltpu.VMEM(full, f32),
+            pltpu.VMEM((4, 128), f32),
+            pltpu.VMEM((1, 128), f32),
         ),
         in_specs=[anywhere] * 5,
         out_specs=(
-            anywhere,
             pl.BlockSpec(memory_space=pltpu.VMEM),
-            pl.BlockSpec(memory_space=pltpu.SMEM),
+            pl.BlockSpec(memory_space=pltpu.VMEM),
+            pl.BlockSpec(memory_space=pltpu.VMEM),
         ),
         scratch_shapes=scratch,
         compiler_params=pltpu.CompilerParams(collective_id=0, has_side_effects=True),
     )(vel, tiles(driving, 2), tiles(observed, 2), tiles(log_friction, 1), tiles(ice_mask, 1))
+    out, fric, misfit = pl.pallas_call(
+        hand_over,
+        out_shape=(
+            jax.ShapeDtypeStruct(full, f32),
+            jax.ShapeDtypeStruct((4, 128), f32),
+            jax.ShapeDtypeStruct((1, 128), f32),
+        ),
+        in_specs=[pl.BlockSpec(memory_space=pltpu.VMEM)] * 3,
+        out_specs=(anywhere,) * 3,
+        scratch_shapes=[dma((3,))],
+    )(*(pltpu.with_memory_space_constraint(a, pltpu.VMEM) for a in (out, fric, misfit)))
     velocity = out.reshape(2, 4, 16, 2, 128).transpose(0, 1, 3, 2, 4).reshape(2, 4, 2, 2048)
     fric = fric.reshape(2, 2, 128).transpose(1, 0, 2).reshape(2, 256)
-    return velocity, fric, misfit.reshape(())
+    return velocity, fric, misfit[0, 0]
 
 
 def solution(mesh):

time: 64.6 us -> 59.2 us (0.916)
  local copies, waits for them, and re-layouts: 2.15 us -> 0 us
  between operations: 2.41 us -> 0.64 us
  Pallas kernels: 59.8 us -> 58.4 us
    unnamed x4 -> x0, local copies, waits for them, and re-layouts: 2.15 us -> none
    pallas_call x1 -> x2, Pallas kernels: 59.8 us -> 58.4 us  [the longest x1 57.8 us: on_device(): pl.pallas_call(kernel, out_shape=(pltpu.VMEM(full, f32), pltpu.VMEM((4, 1...]
where the time goes in v3:
time: 59.2 us; the launch traced here: 59.1 us
  Pallas kernels  58.4 us (99%)
  between operations  0.64 us (1%)
    pallas_call x1, Pallas kernels, on_device(): pl.pallas_call(kernel, out_shape=(pltpu.VMEM(full, f32), pltpu.VMEM((4, 1...  57.8 us

profile of v3, /device:TPU:1, one launch (start us, length us, event | category | flops | bytes accessed | tf_op | source)
XLA Modules:
  0.0 59.1 jit_solution(5876432521685179614)
XLA Ops:
  0.6 57.8 %shard_map.76 = (f32[256,128]{1,0:T(8,128)S(1)}, f32[4,128]{1,0:T(4,128)S(1)}, f32[1,128]{1,0:T(1,128)S(1)}) custom-call(f32[256,128]{1,0:T(8,128)} %bitcast.37, f32[8,128]{1,0:T(8,128)} %bitcast.38, f32[8,128]{1,0:T(8,128)} %bitcast.39, f32[4,128]{1,0:T(4,128)} %bitcast.40, s32[4,128]{1,0:T(4,128)} %bitcast.41), custom_call_target="tpu_custom_call" | custom-call | tf_op jit(solution)/shard_map/pallas_call | solution.py:512
  58.4 0.7 %shard_map.77 = (f32[256,128]{1,0:T(8,128)}, f32[4,128]{1,0:T(4,128)}, f32[1,128]{1,0:T(1,128)}) custom-call(f32[256,128]{1,0:T(8,128)S(1)} %get-tuple-element.9.out, f32[4,128]{1,0:T(4,128)S(1)} %get-tuple-element.10.fric, f32[1,128]{1,0:T(1,128)S(1)} %get-tuple-element.11.misfit), custom_call_target="tpu_custom_call" | custom-call | tf_op jit(solution)/shard_map/pallas_call | solution.py:528

commit v4 on v3

--- a/solution.py
+++ b/solution.py
@@ -43,7 +43,7 @@
     vout, fric_out, misfit_out,
     vin, drv, obs, logf, mask, stage, small, small_in,
     w0, w1, w2, dn0, up0, dn1, up1, am, adn, aup, alow, ahigh,
-    eta_m, eta_r, diag_m, diag_r, rhs_m, rhs_r, ratio_m, ratio_r, val_m, val_r, inv_m, inv_r, rim_x, faces,
+    eta_m, eta_r, diag_m, diag_r, rhs_m, rhs_r, ratio_m, ratio_r, val_m, val_r, inv_m, inv_r, rim_x, faces, cross, flip,
     vel_in, grad, grad_in, row1, row2, sum1, sum2,
     load_sem, a2a_send, a2a_recv, small_send, small_recv, halo_send, halo_recv,
     vel_send, vel_recv, grad_send, grad_recv, s1_send, s1_recv, s2_send, s2_recv, token,
@@ -161,16 +161,20 @@
         pltpu.make_async_copy(ref, ref, sem).wait()
 
     rows = pl.ds(pl.multiple_of(L * SLAB, 8), SLAB)
-    for l in range(SLOTS):
-        remote(stage.at[l * SLAB:l * SLAB + SLAB], w0.at[rows], a2a_send.at[l], a2a_recv.at[L], owners[l])
+    def slots_by_x(order):
+        return [lax.rem(x + dx, 4) * 2 + half for dx in order for half in range(2)]
+
+    for l in slots_by_x((2, 1, 3, 0)):
+        part = pl.ds(pl.multiple_of(l * SLAB, 8), SLAB)
+        remote(stage.at[part], w0.at[rows], a2a_send.at[l], a2a_recv.at[L], owner_of(M, l))
     for side in range(3):
         target = owner_of(M, lax.rem(L + SLOTS + 1 - side, SLOTS))
         remote(small, small_in.at[side], small_send.at[side], small_recv.at[side], target)
 
     take_tokens(0)
     give_tokens(1)
-    for l in range(SLOTS):
-        rows = pl.ds(l * SLAB, SLAB)
+    for l in slots_by_x((0, 1, 3, 2)):
+        rows = pl.ds(pl.multiple_of(l * SLAB, 8), SLAB)
         arrived(w0.at[rows], a2a_recv.at[l])
         for i, (device, land) in enumerate(((below, up0), (above, dn0))):
             pltpu.make_async_remote_copy(
@@ -383,9 +387,26 @@
                 edge[pl.ds(j * 32 + s, 8, stride=4), :] = am[pl.ds(j * 8 + s * 2 + r, 8, stride=SLAB), :]
         pieces(edge, land, 4, (2, r), device)
 
-    arrived(aup, halo_recv.at[2, 0])
-    arrived(adn, halo_recv.at[2, 1])
-
+    def eliminate_unit(slot, prev, steps=range(4)):
+        for kk in steps:
+            k, under = at(slot, kk), at(slot, kk - 1) if kk > 0 else at(slot - 1, 3)
+            prev = (1024.0 * (eta_m[under, :] + eta_m[k, :]) * inv_m[k, :]) * prev
+            val_m[k, :] = prev
+        return prev
+
+    first = inv_m[0:8, :]
+    val_m[0:8, :] = first
+    lax.fori_loop(1, SLOTS, eliminate_unit, eliminate_unit(0, first, range(1, 4)))
+
+    def substitute_unit(i, following):
+        for kk in reversed(range(4)):
+            k = at(SLOTS - 1 - i, kk)
+            following = val_m[k, :] - ratio_m[k, :] * following
+            val_m[k, :] = following
+        return following
+
+    lax.fori_loop(0, SLOTS, substitute_unit, zero)
+    total = [zero] * 8
     for kk in range(4):
         for c in range(2):
             rows = [[am[pl.ds(kk * 8 + c * 4 + t * 2 + r, 8, stride=SLAB), :] for t in range(2)] for r in range(2)]
@@ -394,39 +415,30 @@
             for r in range(2):
                 right, left = ahead(rows[r]), behind(rows[r])
                 for t in range(2):
+                    s = c * 4 + t * 2 + r
+                    weight = val_m[pl.ds(kk * 8 + s, 8, stride=SLAB), :]
+                    east, west, north, south = [faces[kk, (r * 2 + t) * 4 + i] for i in range(4)]
                     if r == 0:
-                        low = adn[pl.ds(kk * 32 + c * 2 + t, 8, stride=4), :] * has_below
-                        high = rows[1][t]
+                        along, outer = east * rows[1][t], west * has_below
                     else:
-                        low = rows[0][t]
-                        high = aup[pl.ds(kk * 32 + c * 2 + t, 8, stride=4), :] * has_above
-                    east, west, north, south = [faces[kk, (r * 2 + t) * 4 + i] for i in range(4)]
-                    along = east * high + west * low
+                        along, outer = west * rows[0][t], east * has_above
                     across = north * right[t] + south * left[t]
                     value = 4.0 * along + across if c == 0 else along + 4.0 * across
-                    rhs_m[pl.ds(kk * 8 + c * 4 + t * 2 + r, 8, stride=SLAB), :] = value
-    rhs_m[top, :] = rhs_m[top, :] + source[0]
-
-    def eliminate_second(slot, prev, steps=range(4)):
-        for kk in steps:
-            k, under = at(slot, kk), at(slot, kk - 1) if kk > 0 else at(slot - 1, 3)
-            lower = 1024.0 * (eta_m[under, :] + eta_m[k, :])
-            inverse = inv_m[k, :]
-            prev = rhs_m[k, :] * inverse + (lower * inverse) * prev
-            val_m[k, :] = prev
-        return prev
-
-    first = rhs_m[0:8, :] * inv_m[0:8, :]
-    val_m[0:8, :] = first
-    lax.fori_loop(1, SLOTS, eliminate_second, eliminate_second(0, first, range(1, 4)))
-
-    def substitute_second(i, following):
-        for kk in reversed(range(4)):
-            k = at(SLOTS - 1 - i, kk)
-            following = val_m[k, :] - ratio_m[k, :] * following
-        return following
-
-    bottom = jnp.where(ice[0], lax.fori_loop(0, SLOTS, substitute_second, zero), 0.0)
+                    total[s] = total[s] + weight * value
+                    cross[kk, s] = weight * (4.0 * outer if c == 0 else outer)
+    ahead_part = val_m[top, :] * source[0]
+
+    arrived(aup, halo_recv.at[2, 0])
+    arrived(adn, halo_recv.at[2, 1])
+    for s in range(8):
+        edge = adn if s % 2 == 0 else aup
+        for kk in range(4):
+            total[s] = total[s] + cross[kk, s] * edge[pl.ds(kk * 32 + s // 2, 8, stride=4), :]
+        flip[s * 8:s * 8 + 8, :] = total[s]
+    bottom = ahead_part
+    for i in range(8):
+        bottom = bottom + flip[pl.ds(i, 8, stride=8), :]
+    bottom = jnp.where(ice[0], bottom, 0.0)
 
     product = w2[0:8, :] * bottom
     gradient = -bed[0][0:4, :] * (product[0:4, :] + product[4:8, :])
@@ -458,6 +470,12 @@
                     for s in range(4):
                         piece = vel_in[pl.ds(kk * 8 + c * 4 + s, 8, stride=SLAB), :]
                         vout[pl.ds((c * 4 + kk) * 32 + s, 8, stride=4), :] = piece
+        if number == 1:
+            for copy in sends:
+                copy.wait_send()
+            bulk += [(w0, halo_send.at[0, i]) for i in range(2)]
+            for src, sem in bulk:
+                arrived(src, sem)
         for other in reversed(others):
             arrived(sum_ref.at[other], recv_sem.at[other])
         parts = [sum_ref[i] for i in range(32)]
@@ -471,12 +489,6 @@
     arrived(grad_in, grad_recv)
     scale = jnp.sqrt(jnp.full((4, 128), grad_total, f32) / COLUMNS + 1e-06)
     fric_out[...] = logf[...] - step_size * grad_in[...] / scale
-
-    for copy in sends:
-        copy.wait_send()
-    bulk += [(w0, halo_send.at[0, i]) for i in range(2)]
-    for src, sem in bulk:
-        arrived(src, sem)
 
 
 def hand_over(out, fric, misfit, out_hbm, fric_hbm, misfit_hbm, sem):
@@ -503,7 +515,7 @@
     scratch = [vm((272, 128)), vm((8, 128)), vm((8, 128)), vm((4, 128)), pltpu.VMEM((4, 128), jnp.int32)]
     scratch += [vm(slab), vm((24, 128)), vm((3, 24, 128))]
     scratch += [vm(slab)] * 8 + [vm(half)] * 4
-    scratch += [vm(slab)] * 13 + [vm((GROUPS, 16, 8, 128))]
+    scratch += [vm(slab)] * 13 + [vm((GROUPS, 16, 8, 128)), vm((GROUPS, 8, 8, 128)), vm((64, 128))]
     scratch += [vm(slab), vm((4, 128)), vm((4, 128))]
     scratch += [vm((1, 128))] * 2 + [vm((32, 1, 128))] * 2
     scratch += [dma((5,)), dma((8,)), dma((8,)), dma((3,)), dma((3,)), dma((3, 2)), dma((3, 2))]

time: 59.2 us -> 57.3 us (0.968)
  Pallas kernels: 58.4 us -> 56.5 us
    pallas_call x1, Pallas kernels: 57.8 us -> 55.8 us  [on_device(): pl.pallas_call(kernel, out_shape=(pltpu.VMEM(full, f32), pltpu.VMEM((4, 1...]
where the time goes in v4:
time: 57.3 us; the launch traced here: 57.2 us
  Pallas kernels  56.5 us (99%)
  between operations  0.64 us (1%)
    pallas_call x1, Pallas kernels, on_device(): pl.pallas_call(kernel, out_shape=(pltpu.VMEM(full, f32), pltpu.VMEM((4, 1...  55.8 us

profile of v4, /device:TPU:1, one launch (start us, length us, event | category | flops | bytes accessed | tf_op | source)
XLA Modules:
  0.0 57.2 jit_solution(624143371512505441)
XLA Ops:
  0.6 55.8 %shard_map.76 = (f32[256,128]{1,0:T(8,128)S(1)}, f32[4,128]{1,0:T(4,128)S(1)}, f32[1,128]{1,0:T(1,128)S(1)}) custom-call(f32[256,128]{1,0:T(8,128)} %bitcast.37, f32[8,128]{1,0:T(8,128)} %bitcast.38, f32[8,128]{1,0:T(8,128)} %bitcast.39, f32[4,128]{1,0:T(4,128)} %bitcast.40, s32[4,128]{1,0:T(4,128)} %bitcast.41), custom_call_target="tpu_custom_call" | custom-call | tf_op jit(solution)/shard_map/pallas_call | solution.py:524
  56.5 0.7 %shard_map.77 = (f32[256,128]{1,0:T(8,128)}, f32[4,128]{1,0:T(4,128)}, f32[1,128]{1,0:T(1,128)}) custom-call(f32[256,128]{1,0:T(8,128)S(1)} %get-tuple-element.9.out, f32[4,128]{1,0:T(4,128)S(1)} %get-tuple-element.10.fric, f32[1,128]{1,0:T(1,128)S(1)} %get-tuple-element.11.misfit), custom_call_target="tpu_custom_call" | custom-call | tf_op jit(solution)/shard_map/pallas_call | solution.py:540

commit v5 on v4

--- a/solution.py
+++ b/solution.py
@@ -30,12 +30,12 @@
     z, y_lo, core = place(m)
     y = lax.rem(l, 2) * 4 + y_lo
     odd = lax.rem(z, 2)
-    return device_at(lax.div(l, 2), lax.rem(odd * (y + 2) + (1 - odd) * (13 - y), 8), z, core)
+    return device_at(lax.div(l, 2), lax.rem((1 - odd) * (y + 2) + odd * (13 - y), 8), z, core)
 
 
 def block_of(x, y, z, core):
     odd = lax.rem(z, 2)
-    return device_at(x, lax.rem(odd * (y + 6) + (1 - odd) * (13 - y), 8), z, core)
+    return device_at(x, lax.rem((1 - odd) * (y + 6) + odd * (13 - y), 8), z, core)
 
 
 def kernel(
@@ -65,7 +65,13 @@
     bm, bl = block_of(x, y, z, core)
     below = owner_of(lax.rem(bm + BLOCKS - 1, BLOCKS), bl)
     above = owner_of(lax.rem(bm + 1, BLOCKS), bl)
-    owners = [owner_of(M, jnp.int32(l)) for l in range(SLOTS)]
+    own_map, own_half = owner_of(M, jnp.int32(0))
+    flip_half = 1 - 2 * own_half
+
+    def owner_in_row(column, half):
+        return own_map, column * 2 + own_half + half * flip_half
+
+    owners = [owner_in_row(jnp.int32(column), half) for column in range(4) for half in range(2)]
     holders = [(bm, jnp.int32(l)) for l in range(SLOTS)]
 
     def peer_z(j):
@@ -147,15 +153,14 @@
 
     bulk = []
 
-    def pieces(src, dst, count, index, device):
+    def pieces(src, dst, count, index, device, first, length):
         size = src.shape[0] // count
         for i in reversed(range(count)):
-            rows = pl.ds(i * size, size)
+            rows = pl.ds(i * size + first, length)
             pltpu.make_async_remote_copy(
                 src_ref=src.at[rows], dst_ref=dst.at[rows], send_sem=halo_send.at[index],
                 recv_sem=halo_recv.at[index], device_id=device, device_id_type=MESH,
             ).start()
-        bulk.append((src, halo_send.at[index]))
 
     def arrived(ref, sem):
         pltpu.make_async_copy(ref, ref, sem).wait()
@@ -164,9 +169,12 @@
     def slots_by_x(order):
         return [lax.rem(x + dx, 4) * 2 + half for dx in order for half in range(2)]
 
-    for l in slots_by_x((2, 1, 3, 0)):
-        part = pl.ds(pl.multiple_of(l * SLAB, 8), SLAB)
-        remote(stage.at[part], w0.at[rows], a2a_send.at[l], a2a_recv.at[L], owner_of(M, l))
+    for dx in (2, 1, 3, 0):
+        column = lax.rem(x + dx, 4)
+        for half in range(2):
+            l = column * 2 + half
+            part = pl.ds(pl.multiple_of(l * SLAB, 8), SLAB)
+            remote(stage.at[part], w0.at[rows], a2a_send.at[l], a2a_recv.at[L], owner_in_row(column, half))
     for side in range(3):
         target = owner_of(M, lax.rem(L + SLOTS + 1 - side, SLOTS))
         remote(small, small_in.at[side], small_send.at[side], small_recv.at[side], target)
@@ -349,9 +357,12 @@
         arrived(land, halo_recv.at[0, i])
     forward_terms(w0, dn0, up0)
     solve(w1)
+    for i, (device, land) in enumerate(((below, up1), (above, dn1))):
+        pieces(w1, land, SLOTS, (1, i), device, 0, 32)
+        bulk.append((w1, halo_send.at[1, i]))
     pack_rims(w1)
     for i, (device, land) in enumerate(((below, up1), (above, dn1))):
-        pieces(w1, land, SLOTS, (1, i), device)
+        pieces(w1, land, SLOTS, (1, i), device, 32, 8)
 
     for i, land in enumerate((up1, dn1)):
         arrived(land, halo_recv.at[1, i])
@@ -385,7 +396,8 @@
         for s in range(4):
             for j in range(GROUPS):
                 edge[pl.ds(j * 32 + s, 8, stride=4), :] = am[pl.ds(j * 8 + s * 2 + r, 8, stride=SLAB), :]
-        pieces(edge, land, 4, (2, r), device)
+        pieces(edge, land, 4, (2, r), device, 0, 32)
+        bulk.append((edge, halo_send.at[2, r]))
 
     def eliminate_unit(slot, prev, steps=range(4)):
         for kk in steps:

time: 57.3 us -> 56.2 us (0.981)
  Pallas kernels: 56.5 us -> 55.4 us
    pallas_call x1, Pallas kernels: 55.8 us -> 54.8 us  [on_device(): pl.pallas_call(kernel, out_shape=(pltpu.VMEM(full, f32), pltpu.VMEM((4, 1...]
where the time goes in v5:
time: 56.2 us; the launch traced here: 56.1 us
  Pallas kernels  55.4 us (99%)
  between operations  0.64 us (1%)
    pallas_call x1, Pallas kernels, on_device(): pl.pallas_call(kernel, out_shape=(pltpu.VMEM(full, f32), pltpu.VMEM((4, 1...  54.8 us

profile of v5, /device:TPU:1, one launch (start us, length us, event | category | flops | bytes accessed | tf_op | source)
XLA Modules:
  0.0 56.1 jit_solution(18243698863880444734)
XLA Ops:
  0.6 54.8 %shard_map.76 = (f32[256,128]{1,0:T(8,128)S(1)}, f32[4,128]{1,0:T(4,128)S(1)}, f32[1,128]{1,0:T(1,128)S(1)}) custom-call(f32[256,128]{1,0:T(8,128)} %bitcast.37, f32[8,128]{1,0:T(8,128)} %bitcast.38, f32[8,128]{1,0:T(8,128)} %bitcast.39, f32[4,128]{1,0:T(4,128)} %bitcast.40, s32[4,128]{1,0:T(4,128)} %bitcast.41), custom_call_target="tpu_custom_call" | custom-call | tf_op jit(solution)/shard_map/pallas_call | solution.py:536
  55.4 0.7 %shard_map.77 = (f32[256,128]{1,0:T(8,128)}, f32[4,128]{1,0:T(4,128)}, f32[1,128]{1,0:T(1,128)}) custom-call(f32[256,128]{1,0:T(8,128)S(1)} %get-tuple-element.9.out, f32[4,128]{1,0:T(4,128)S(1)} %get-tuple-element.10.fric, f32[1,128]{1,0:T(1,128)S(1)} %get-tuple-element.11.misfit), custom_call_target="tpu_custom_call" | custom-call | tf_op jit(solution)/shard_map/pallas_call | solution.py:552

commit v6 on v5

--- a/solution.py
+++ b/solution.py
@@ -328,7 +328,7 @@
             return carry
 
         carry = tuple((zero, zero, zero, bed[part]) for part in range(2))
-        carry = lax.fori_loop(0, SLOTS - 1, eliminate, carry)
+        carry = lax.fori_loop(0, SLOTS - 1, eliminate, carry, unroll=True)
         eliminate(SLOTS - 1, carry, last=True)
 
         def substitute(i, following):
@@ -344,7 +344,7 @@
                 following = tuple(new)
             return following
 
-        lax.fori_loop(0, SLOTS, substitute, (zero, zero))
+        lax.fori_loop(0, SLOTS, substitute, (zero, zero), unroll=True)
 
     def pack_rims(out):
         for q in range(2):

time: 56.2 us -> 56 us (level)
  no operation moved by 1% of the time
where the time goes in v6:
time: 56 us; the launch traced here: 55.8 us
  Pallas kernels  55.2 us (99%)
  between operations  0.64 us (1%)
    pallas_call x1, Pallas kernels, on_device(): pl.pallas_call(kernel, out_shape=(pltpu.VMEM(full, f32), pltpu.VMEM((4, 1...  54.5 us

profile of v6, /device:TPU:1, one launch (start us, length us, event | category | flops | bytes accessed | tf_op | source)
XLA Modules:
  0.0 55.8 jit_solution(11178680437038257998)
XLA Ops:
  0.6 54.5 %shard_map.76 = (f32[256,128]{1,0:T(8,128)S(1)}, f32[4,128]{1,0:T(4,128)S(1)}, f32[1,128]{1,0:T(1,128)S(1)}) custom-call(f32[256,128]{1,0:T(8,128)} %bitcast.37, f32[8,128]{1,0:T(8,128)} %bitcast.38, f32[8,128]{1,0:T(8,128)} %bitcast.39, f32[4,128]{1,0:T(4,128)} %bitcast.40, s32[4,128]{1,0:T(4,128)} %bitcast.41), custom_call_target="tpu_custom_call" | custom-call | tf_op jit(solution)/shard_map/pallas_call | solution.py:536
  55.1 0.7 %shard_map.77 = (f32[256,128]{1,0:T(8,128)}, f32[4,128]{1,0:T(4,128)}, f32[1,128]{1,0:T(1,128)}) custom-call(f32[256,128]{1,0:T(8,128)S(1)} %get-tuple-element.9.out, f32[4,128]{1,0:T(4,128)S(1)} %get-tuple-element.10.fric, f32[1,128]{1,0:T(1,128)S(1)} %get-tuple-element.11.misfit), custom_call_target="tpu_custom_call" | custom-call | tf_op jit(solution)/shard_map/pallas_call | solution.py:552
